TPU v7x, 128 devices: a whole 4x4x4 slice. The times are simulated.
128 devices in a mesh: grp: 4 (over y), dev: 32 (over x, z, core).
Axes of the slice: x: 4, y: 4, z: 4, core: 2. Of those that a mesh axis runs over, the one named last changes fastest.
Arguments:
- slab: float32 [4096, 64, 512], P(('grp', 'dev')), may hold values from -40 to 40
- start: float32 [512, 256], replicated, may hold values from -0.25 to 0.25
Outputs:
- next_unfolding: float32 [64, 4096, 256], P('dev', 'grp')
- basis: float32 [512, 256], replicated
All inputs are finite; a program needn't handle non-finite values.
Results may differ from a plain program's by a relative error of at most 0.00023.
Values sent between devices are 32-bit elements; how exact they have to be, the bound alone decides.
A program may use at most 64 MiB of HBM per device.

v0:
```python
import jax
import jax.numpy as jnp
from jax import lax
from jax.sharding import Mesh
from jax.sharding import PartitionSpec as P

ITERS = 4
DEV = ("dev_0", "dev_1", "dev_2")
GRP_DEV = ("grp", "dev_0", "dev_1", "dev_2")


def in_blocks(shard, dim, peers):
    before, after = (shard.shape[:dim], shard.shape[dim + 1 :])
    return jnp.moveaxis(shard.reshape(*before, peers, -1, *after), dim, 0)


def summed_on_arrival(shard, axis, dim):
    peers = lax.axis_size(axis)
    blocks = lax.all_to_all(in_blocks(shard, dim, peers), axis, 0, 0, tiled=True)
    return jnp.sum(blocks, axis=0)


def sum_by_axis(shard, axes, dim):
    far, near = axes
    blocks = in_blocks(shard, dim, lax.axis_size(far))
    nearer = summed_on_arrival(blocks, near, dim + 1)
    arrived = lax.all_to_all(nearer, far, split_axis=0, concat_axis=0, tiled=True)
    return arrived.sum(axis=0)


def rows_for(lines, peers):
    spare = -lines.shape[0] % peers
    if not spare:
        return lines
    return jnp.concatenate([lines, jnp.zeros((spare, *lines.shape[1:]), lines.dtype)])


def copy_for_each(shard, axis):
    peers = lax.axis_size(axis)
    return lax.all_to_all(
        jnp.broadcast_to(shard[None], (peers, *shard.shape)), axis, 0, 0, tiled=True
    )


def laid_out(blocks, dim):
    shape = list(blocks.shape[1:])
    shape[dim] *= blocks.shape[0]
    return jnp.moveaxis(blocks, 0, dim).reshape(shape)


def gather_axes(shard, axes, dim):
    far, near = axes
    initial = copy_for_each(shard, far)
    blocks = jnp.swapaxes(copy_for_each(initial, near), 0, 1)
    return laid_out(blocks.reshape(-1, *shard.shape), dim)


def total_of(shard, axes):
    lines = shard.reshape(-1, shard.shape[-1])
    own = sum_by_axis(rows_for(lines, lax.axis_size(axes[0]) * lax.axis_size(axes[1])), axes, 0)
    whole = gather_axes(own, axes, 0)
    return whole[: len(lines)].reshape(shard.shape)


def on_device(slab, start):
    highest = lax.Precision.HIGHEST
    a_local, points, columns = slab.shape
    matrix = slab.reshape(a_local * points, columns)
    scale = jnp.float32(1.0 / (a_local * points * lax.axis_size("grp") * lax.axis_size(DEV)))
    local_gram = jnp.dot(matrix.T, matrix, precision=highest) * scale
    gram = total_of(local_gram, (("grp", "dev_0", "dev_1"), "dev_2"))
    basis = start
    for step in range(ITERS):
        product = jnp.dot(gram, basis, precision=highest)
        lower = jnp.linalg.cholesky(jnp.dot(product.T, product, precision=highest))
        basis = lax.linalg.triangular_solve(
            lower, product, left_side=False, lower=True, transpose_a=True
        )
    projected = jnp.einsum("abk,kr->bar", slab, basis, precision=highest)
    regrouped = lax.all_to_all(projected, DEV, split_axis=0, concat_axis=1, tiled=True)
    return (regrouped, basis)


def solution(mesh):
    torus = Mesh(
        mesh.devices.reshape(mesh.shape["grp"], 4, 4, 2), ("grp", "dev_0", "dev_1", "dev_2")
    )
    return jax.shard_map(
        on_device,
        mesh=torus,
        in_specs=(P(GRP_DEV, None, None), P()),
        out_specs=(P(DEV, "grp", None), P()),
        check_vma=False,
    )
```

profile of v0, /device:TPU:1, one launch (start us, length us, event | category | flops | bytes accessed | tf_op | source)
XLA Modules:
  0.0 364.9 jit_solution(6195941838536461829)
XLA Ops:
  0.6 9.4 %fusion = f32[512,512]{1,0:T(8,128)S(1)} fusion(f32[32,64,512]{2,1,0:T(8,128)} %param.5), kind=kOutput, calls=%fused_computation.10 | convolution fusion | flops 6442713088 | bytes 5242880 | tf_op jit(solution)/shard_map/dot_general | solution.py:70
  11.4 5.0 %all-to-all-start = ((f32[2,64,4,512]{3,2,1,0:T(4,128)}), f32[2,64,4,512]{3,2,1,0:T(4,128)S(1)}, u32[]{:S(2)}, u32[]{:S(2)}) async-start(f32[2,64,4,512]{3,2,1,0:T(4,128)} %bitcast.136), calls=%async_computation | async-start | bytes 2097152 | tf_op jit(solution)/shard_map/all_to_all | solution.py:19
  18.5 23.3 %all_to_all.39 = f32[64,4,512]{2,1,0:T(4,128)S(1)} all-to-all(f32[64,4,512]{2,1,0:T(4,128)S(1)} %reduce_sum.18), channel_id=1, replica_groups=mesh['grp'=4,'dev_0'=4,'dev_1'=4,'dev_2'=2] {'grp','dev_0','dev_1'}, dimensions={0} | all-to-all | bytes 1048576 | tf_op jit(solution)/shard_map/all_to_all | solution.py:27
  42.8 4.7 %all-to-all-start.2 = ((f32[64,4,512]{2,1,0:T(4,128)}), f32[64,4,512]{2,1,0:T(4,128)S(1)}, u32[]{:S(2)}, u32[]{:S(2)}) async-start(f32[64,4,512]{2,1,0:T(4,128)} %broadcast_in_dim.4), calls=%async_computation.2 | async-start | bytes 1048576 | tf_op jit(solution)/shard_map/all_to_all | solution.py:40
  47.5 11.0 %all-to-all-done.2 = f32[64,4,512]{2,1,0:T(4,128)S(1)} async-done(((f32[64,4,512]{2,1,0:T(4,128)}), f32[64,4,512]{2,1,0:T(4,128)S(1)}, u32[]{:S(2)}, u32[]{:S(2)}) %all-to-all-start.2) | async-done | bytes 524320 | tf_op jit(solution)/shard_map/all_to_all | solution.py:40
  58.7 7.4 %all_to_all.38 = f32[2,64,4,512]{3,2,1,0:T(4,128)S(1)} all-to-all(f32[2,64,4,512]{3,2,1,0:T(4,128)S(1)} %broadcast_in_dim.5), channel_id=1, replica_groups=mesh['grp'=4,'dev_0'=4,'dev_1'=4,'dev_2'=2] {'dev_2'}, dimensions={0} | all-to-all | bytes 2097152 | tf_op jit(solution)/shard_map/all_to_all | solution.py:40
  68.8 11.7 %cholesky.214 = f32[128,128]{1,0:T(8,128)S(1)} custom-call(f32[128,128]{1,0:T(8,128)S(1)} %cholesky.346), custom_call_target="Cholesky" | custom-call | tf_op jit(solution)/shard_map/jit(cholesky)/cholesky | solution.py:75
  80.6 9.8 %custom-call.17 = f32[1,128,128]{1,2,0:T(8,128)S(1)} custom-call(f32[1,128,128]{2,1,0:T(8,128)S(1)} %get-tuple-element.99), custom_call_target="InvertDiagBlocksLowerTriangular" | custom-call | tf_op jit(solution)/shard_map/jit(cholesky)/cholesky | solution.py:75
  90.9 12.1 %cholesky.231 = f32[128,128]{1,0:T(8,128)S(1)} custom-call(f32[128,128]{1,0:T(8,128)S(1)} %convolution_subtract_fusion.7), custom_call_target="Cholesky" | custom-call | tf_op jit(solution)/shard_map/jit(cholesky)/cholesky | solution.py:75
  109.1 19.7 %custom-call.18 = f32[2,128,128]{1,2,0:T(8,128)S(1)} custom-call(f32[2,128,128]{2,1,0:T(8,128)S(1)} %get-tuple-element.30), custom_call_target="InvertDiagBlocksLowerTriangular" | custom-call | tf_op jit(solution)/shard_map/triangular_solve/custom-call.0 | solution.py:76
  132.5 11.7 %cholesky.248 = f32[128,128]{1,0:T(8,128)S(1)} custom-call(f32[128,128]{1,0:T(8,128)S(1)} %cholesky.349), custom_call_target="Cholesky" | custom-call | tf_op jit(solution)/shard_map/jit(cholesky)/cholesky | solution.py:75
  144.9 9.8 %custom-call.19 = f32[1,128,128]{1,2,0:T(8,128)S(1)} custom-call(f32[1,128,128]{2,1,0:T(8,128)S(1)} %get-tuple-element.95), custom_call_target="InvertDiagBlocksLowerTriangular" | custom-call | tf_op jit(solution)/shard_map/jit(cholesky)/cholesky | solution.py:75
  155.2 11.9 %cholesky.265 = f32[128,128]{1,0:T(8,128)S(1)} custom-call(f32[128,128]{1,0:T(8,128)S(1)} %convolution_subtract_fusion.6), custom_call_target="Cholesky" | custom-call | tf_op jit(solution)/shard_map/jit(cholesky)/cholesky | solution.py:75
  173.1 19.7 %custom-call.20 = f32[2,128,128]{1,2,0:T(8,128)S(1)} custom-call(f32[2,128,128]{2,1,0:T(8,128)S(1)} %get-tuple-element.31), custom_call_target="InvertDiagBlocksLowerTriangular" | custom-call | tf_op jit(solution)/shard_map/triangular_solve/custom-call.0 | solution.py:76
  196.5 11.7 %cholesky.282 = f32[128,128]{1,0:T(8,128)S(1)} custom-call(f32[128,128]{1,0:T(8,128)S(1)} %cholesky.352), custom_call_target="Cholesky" | custom-call | tf_op jit(solution)/shard_map/jit(cholesky)/cholesky | solution.py:75
  208.9 9.8 %custom-call.21 = f32[1,128,128]{1,2,0:T(8,128)S(1)} custom-call(f32[1,128,128]{2,1,0:T(8,128)S(1)} %get-tuple-element.91), custom_call_target="InvertDiagBlocksLowerTriangular" | custom-call | tf_op jit(solution)/shard_map/jit(cholesky)/cholesky | solution.py:75
  219.2 12.1 %cholesky.299 = f32[128,128]{1,0:T(8,128)S(1)} custom-call(f32[128,128]{1,0:T(8,128)S(1)} %convolution_subtract_fusion.5), custom_call_target="Cholesky" | custom-call | tf_op jit(solution)/shard_map/jit(cholesky)/cholesky | solution.py:75
  237.1 19.7 %custom-call.22 = f32[2,128,128]{1,2,0:T(8,128)S(1)} custom-call(f32[2,128,128]{2,1,0:T(8,128)S(1)} %get-tuple-element.32), custom_call_target="InvertDiagBlocksLowerTriangular" | custom-call | tf_op jit(solution)/shard_map/triangular_solve/custom-call.0 | solution.py:76
  260.5 11.7 %cholesky.316 = f32[128,128]{1,0:T(8,128)S(1)} custom-call(f32[128,128]{1,0:T(8,128)S(1)} %cholesky.355), custom_call_target="Cholesky" | custom-call | tf_op jit(solution)/shard_map/jit(cholesky)/cholesky | solution.py:75
  272.9 9.8 %custom-call.23 = f32[1,128,128]{1,2,0:T(8,128)S(1)} custom-call(f32[1,128,128]{2,1,0:T(8,128)S(1)} %get-tuple-element.87), custom_call_target="InvertDiagBlocksLowerTriangular" | custom-call | tf_op jit(solution)/shard_map/jit(cholesky)/cholesky | solution.py:75
  283.2 11.9 %cholesky.333 = f32[128,128]{1,0:T(8,128)S(1)} custom-call(f32[128,128]{1,0:T(8,128)S(1)} %convolution_subtract_fusion.4), custom_call_target="Cholesky" | custom-call | tf_op jit(solution)/shard_map/jit(cholesky)/cholesky | solution.py:75
  301.3 19.7 %custom-call.24 = f32[2,128,128]{1,2,0:T(8,128)S(1)} custom-call(f32[2,128,128]{2,1,0:T(8,128)S(1)} %get-tuple-element.33), custom_call_target="InvertDiagBlocksLowerTriangular" | custom-call | tf_op jit(solution)/shard_map/triangular_solve/custom-call.0 | solution.py:76
  322.5 5.8 %convolution_bitcast_fusion = f32[64,32,256]{2,0,1:T(8,128)S(1)} fusion(f32[32,64,512]{2,1,0:T(8,128)} %param.5, f32[512,128]{0,1:T(8,128)S(1)} %fusion.26, f32[512,128]{0,1:T(8,128)S(1)} %bitcast.163), kind=kOutput, calls=%fused_computation.8 | convolution fusion | flops 3221356544 | bytes 6815744 | tf_op jit(solution)/shard_map/abk,kr->bar/dot_general | solution.py:79
  337.7 25.6 %all-to-all-done.4 = f32[64,32,256]{2,1,0:T(8,128)S(1)} async-done(((f32[64,32,256]{2,1,0:T(8,128)}), f32[64,32,256]{2,1,0:T(8,128)S(1)}, u32[]{:S(2)}, u32[]{:S(2)}) %all-to-all-start.4) | async-done | bytes 2097184 | tf_op jit(solution)/shard_map/all_to_all | solution.py:80
  (113 shorter events, 69.3 us)
Async XLA Ops:
  0.6 66.0 %copy-start = (f32[512,256]{1,0:T(8,128)S(1)}, f32[512,256]{1,0:T(8,128)}, u32[]{:S(2)}) copy-start(f32[512,256]{1,0:T(8,128)} %param.6) | copy-start | bytes 1572868
  11.4 6.7 %all-to-all-start = ((f32[2,64,4,512]{3,2,1,0:T(4,128)}), f32[2,64,4,512]{3,2,1,0:T(4,128)S(1)}, u32[]{:S(2)}, u32[]{:S(2)}) async-start(f32[2,64,4,512]{3,2,1,0:T(4,128)} %bitcast.136), calls=%async_computation | async-start | bytes 2097152 | tf_op jit(solution)/shard_map/all_to_all | solution.py:19
  42.8 15.7 %all-to-all-start.2 = ((f32[64,4,512]{2,1,0:T(4,128)}), f32[64,4,512]{2,1,0:T(4,128)S(1)}, u32[]{:S(2)}, u32[]{:S(2)}) async-start(f32[64,4,512]{2,1,0:T(4,128)} %broadcast_in_dim.4), calls=%async_computation.2 | async-start | bytes 1048576 | tf_op jit(solution)/shard_map/all_to_all | solution.py:40
  330.8 32.5 %all-to-all-start.4 = ((f32[64,32,256]{2,1,0:T(8,128)}), f32[64,32,256]{2,1,0:T(8,128)S(1)}, u32[]{:S(2)}, u32[]{:S(2)}) async-start(f32[64,32,256]{2,1,0:T(8,128)} %copy.46), calls=%async_computation.4 | async-start | bytes 4194304 | tf_op jit(solution)/shard_map/all_to_all | solution.py:80
where the time goes:
time: 371 us; the launch traced here: 365 us
  other arithmetic  219 us (59%)
  waiting for transfers between devices  38.3 us (10%)
  matrix products  30.9 us (8%)
  blocking collectives  30.7 us (8%)
  local copies, waits for them, and re-layouts  25.3 us (7%)
  starting transfers between devices  13.7 us (4%)
  between operations  6.51 us (2%)
    another operation x27, other arithmetic, on_device(): lower = jnp.linalg.cholesky(jnp.dot(product.T, product, precision=highest))  139 us
    another operation x10, other arithmetic, on_device(): lax.linalg.triangular_solve(lower, product, left_side=False, lower=True,...  79.6 us
    all_to_all x1, waiting for transfers between devices, on_device(): lax.all_to_all(projected, DEV, split_axis=0, concat_axis=1, tiled=True)  25.6 us
    all_to_all x1, blocking collectives, sum_by_axis(): lax.all_to_all(nearer, far, split_axis=0, concat_axis=0, tiled=True)  23.3 us
    another operation x29, local copies, waits for them, and re-layouts, on_device(): lax.linalg.triangular_solve(lower, product, left_side=False, lower=True,...  15.8 us
    all_to_all x1, waiting for transfers between devices, copy_for_each(): lax.all_to_all(jnp.broadcast_to(shard[None], (peers, *shard.shape)), axis...  11 us
    dot_general x1, matrix products, on_device(): local_gram = jnp.dot(matrix.T, matrix, precision=highest) * scale  9.38 us
  transfers between devices with their start and end apart: 3, of which 3 were waited for; matrix products, arithmetic and copies ran while one was open for 1% of the time, Pallas kernels for 0%

commit v1 on v0

--- a/solution.py
+++ b/solution.py
@@ -1,6 +1,8 @@
 import jax
 import jax.numpy as jnp
 from jax import lax
+from jax.experimental import pallas as pl
+from jax.experimental.pallas import tpu as pltpu
 from jax.sharding import Mesh
 from jax.sharding import PartitionSpec as P
 
@@ -62,6 +64,109 @@
     return whole[: len(lines)].reshape(shard.shape)
 
 
+HIGHEST = lax.Precision.HIGHEST
+BLOCK = 64
+
+
+def contract(a, b, dim_a, dim_b):
+    return lax.dot_general(
+        a, b, (((dim_a,), (dim_b,)), ((), ())), precision=HIGHEST, preferred_element_type=jnp.float32
+    )
+
+
+def inverse_factor(block):
+    size = block.shape[0]
+    diagonal = lax.broadcasted_iota(jnp.int32, (size, size), 0) == lax.broadcasted_iota(jnp.int32, (size, size), 1)
+    both = jnp.concatenate([block, diagonal.astype(jnp.float32)], axis=1)
+    wide = (8, 2 * size)
+    count = size // 8
+    tiles = [both[8 * t : 8 * t + 8, :] for t in range(count)]
+    row_of = lax.broadcasted_iota(jnp.int32, wide, 0)
+    for t in range(count):
+        cols = [[jnp.broadcast_to(tiles[u][:, 8 * t + c : 8 * t + c + 1], wide) for u in range(t, count)] for c in range(8)]
+        rows = [jnp.broadcast_to(tiles[t][i : i + 1, :], wide) for i in range(8)]
+        a = [
+            [
+                jnp.broadcast_to(jnp.sum(jnp.where(row_of == i, cols[c][0], 0.0), axis=0, keepdims=True), wide)
+                if i >= c
+                else None
+                for c in range(8)
+            ]
+            for i in range(8)
+        ]
+        unit = [[None] * 8 for _ in range(8)]
+        scaled = []
+        for c in range(8):
+            inverse = 1.0 / a[c][c]
+            for i in range(c + 1, 8):
+                unit[i][c] = a[i][c] * inverse
+            for k in range(c + 1, 8):
+                for i in range(k, 8):
+                    a[i][k] = a[i][k] - unit[i][c] * a[k][c]
+            for i in range(c + 1, 8):
+                rows[i] = rows[i] - unit[i][c] * rows[c]
+            scaled.append(rows[c] * inverse)
+        for u in range(t + 1, count):
+            col = [cols[c][u - t] for c in range(8)]
+            for c in range(8):
+                for k in range(c + 1, 8):
+                    col[k] = col[k] - unit[k][c] * col[c]
+            change = col[0] * scaled[0]
+            for c in range(1, 8):
+                change = change + col[c] * scaled[c]
+            tiles[u] = tiles[u] - change
+        for c in range(8):
+            tiles[t] = jnp.where(row_of == c, rows[c] * lax.rsqrt(a[c][c]), tiles[t])
+    return jnp.concatenate(tiles, axis=0)[:, size:]
+
+
+def inverse_cholesky(m_ref, v_ref):
+    size = m_ref.shape[0]
+    v_ref[...] = jnp.zeros_like(v_ref)
+    for lo in range(0, size, BLOCK):
+        hi = lo + BLOCK
+        inner = inverse_factor(m_ref[lo:hi, lo:hi])
+        if lo:
+            v_ref[lo:hi, :lo] = contract(inner, v_ref[lo:hi, :lo], 1, 0)
+        v_ref[lo:hi, lo:hi] = inner
+        if hi < size:
+            across = contract(inner, m_ref[lo:hi, hi:], 1, 0)
+            down = contract(m_ref[hi:, lo:hi], inner, 1, 1)
+            m_ref[hi:, hi:] -= contract(down, across, 1, 0)
+            v_ref[hi:, :hi] -= contract(down, v_ref[lo:hi, :hi], 1, 0)
+
+
+def iterate(gram_ref, start_ref, basis_ref, rows_ref, product_ref, m_ref, v_ref):
+    rows_ref[...] = start_ref[...].T
+
+    def step(_, carry):
+        product_ref[...] = contract(rows_ref[...], gram_ref[...], 1, 0)
+        m_ref[...] = contract(product_ref[...], product_ref[...], 1, 1)
+        inverse_cholesky(m_ref, v_ref)
+        rows_ref[...] = contract(v_ref[...], product_ref[...], 1, 0)
+        return carry
+
+    lax.fori_loop(0, ITERS, step, 0)
+    basis_ref[...] = rows_ref[...].T
+
+
+def subspace(gram, start):
+    columns, rank = start.shape
+    return pl.pallas_call(
+        iterate,
+        out_shape=jax.ShapeDtypeStruct((columns, rank), jnp.float32),
+        in_specs=[pl.BlockSpec(memory_space=pltpu.VMEM)] * 2,
+        out_specs=pl.BlockSpec(memory_space=pltpu.VMEM),
+        scratch_shapes=[
+            pltpu.VMEM((rank, columns), jnp.float32),
+            pltpu.VMEM((rank, columns), jnp.float32),
+            pltpu.VMEM((rank, rank), jnp.float32),
+            pltpu.VMEM((rank, rank), jnp.float32),
+        ],
+        name="subspace",
+    )(gram, start)
+
+
 def on_device(slab, start):
     highest = lax.Precision.HIGHEST
     a_local, points, columns = slab.shape
@@ -69,13 +174,7 @@
     scale = jnp.float32(1.0 / (a_local * points * lax.axis_size("grp") * lax.axis_size(DEV)))
     local_gram = jnp.dot(matrix.T, matrix, precision=highest) * scale
     gram = total_of(local_gram, (("grp", "dev_0", "dev_1"), "dev_2"))
-    basis = start
-    for step in range(ITERS):
-        product = jnp.dot(gram, basis, precision=highest)
-        lower = jnp.linalg.cholesky(jnp.dot(product.T, product, precision=highest))
-        basis = lax.linalg.triangular_solve(
-            lower, product, left_side=False, lower=True, transpose_a=True
-        )
+    basis = subspace(gram, start)
     projected = jnp.einsum("abk,kr->bar", slab, basis, precision=highest)
     regrouped = lax.all_to_all(projected, DEV, split_axis=0, concat_axis=1, tiled=True)
     return (regrouped, basis)

time: 371 us -> 152 us (0.41); the launches traced: 365 us -> 152 us
  other arithmetic: 219 us -> 0.55 us
  blocking collectives: 30.7 us -> 83.3 us
  Pallas kernels: 0 us -> 47.5 us
  waiting for transfers between devices: 38.3 us -> 0 us
  local copies, waits for them, and re-layouts: 25.3 us -> 4.74 us
  matrix products: 30.9 us -> 15.2 us
  starting transfers between devices: 13.7 us -> 0 us
  between operations: 6.51 us -> 0.69 us
    another operation x37 -> x0, other arithmetic: 219 us -> none  [the longest x27 139 us: on_device(): lower = jnp.linalg.cholesky(jnp.dot(product.T, product, precision=highest))]
    pallas_call x0 -> x1, Pallas kernels: none -> 47.5 us  [subspace(): pl.pallas_call(iterate, out_shape=jax.ShapeDtypeStruct((columns, rank), j...]
    all_to_all x3 -> x0, waiting for transfers between devices: 38.3 us -> none  [the longest x1 25.6 us: on_device(): lax.all_to_all(projected, DEV, split_axis=0, concat_axis=1, tiled=True)]
    all_to_all x0 -> x2, blocking collectives: none -> 37.1 us  [the longest x1 31.5 us: on_device(): lax.all_to_all(projected, DEV, split_axis=0, concat_axis=1, tiled=True)]
    another operation x37 -> x0, local copies, waits for them, and re-layouts: 15.9 us -> none  [the longest x29 15.8 us: on_device(): lax.linalg.triangular_solve(lower, product, left_side=False, lower=True,...]
    all_to_all x1 -> x2, blocking collectives: 7.39 us -> 23 us  [copy_for_each(): lax.all_to_all(jnp.broadcast_to(shard[None], (peers, *shard.shape)), axis...]
    all_to_all x3 -> x0, starting transfers between devices: 13.7 us -> none  [the longest x1 4.95 us: summed_on_arrival(): lax.all_to_all(in_blocks(shard, dim, peers), axis, 0, 0, tiled=True)]
    dot_general x8 -> x0, matrix products: 8.13 us -> none  [the longest x4 4.08 us: on_device(): lower = jnp.linalg.cholesky(jnp.dot(product.T, product, precision=highest))]
  transfers between devices with their start and end apart: 3 -> 0, of which waited for: 3 -> 0; matrix products, arithmetic and copies ran while one was open for 1% -> 0% of each run, Pallas kernels for 0% -> 0%
where the time goes in v1:
time: 152 us
  blocking collectives  83.3 us (55%)
  Pallas kernels  47.5 us (31%)
  matrix products  15.2 us (10%)
  local copies, waits for them, and re-layouts  4.74 us (3%)
    pallas_call x1, Pallas kernels, subspace(): pl.pallas_call(iterate, out_shape=jax.ShapeDtypeStruct((columns, rank), j...  47.5 us
    all_to_all x1, blocking collectives, on_device(): lax.all_to_all(projected, DEV, split_axis=0, concat_axis=1, tiled=True)  31.5 us
    all_to_all x1, blocking collectives, sum_by_axis(): lax.all_to_all(nearer, far, split_axis=0, concat_axis=0, tiled=True)  23.3 us
    all_to_all x2, blocking collectives, copy_for_each(): lax.all_to_all(jnp.broadcast_to(shard[None], (peers, *shard.shape)), axis...  23 us
    dot_general x1, matrix products, on_device(): local_gram = jnp.dot(matrix.T, matrix, precision=highest) * scale  9.33 us
    dot_general x1, matrix products, on_device(): projected = jnp.einsum('abk,kr->bar', slab, basis, precision=highest)  5.84 us
    all_to_all x1, blocking collectives, summed_on_arrival(): lax.all_to_all(in_blocks(shard, dim, peers), axis, 0, 0, tiled=True)  5.58 us

profile of v1, /device:TPU:1, one launch (start us, length us, event | category | flops | bytes accessed | tf_op | source)
XLA Modules:
  0.0 152.0 jit_solution(9220688072217814554)
XLA Ops:
  0.6 9.3 %fusion = f32[512,512]{1,0:T(8,128)S(1)} fusion(f32[32,64,512]{2,1,0:T(8,128)} %param.2), kind=kOutput, calls=%fused_computation.2 | convolution fusion | flops 6442713088 | bytes 5242880 | tf_op jit(solution)/shard_map/dot_general | solution.py:175
  10.0 0.3 reshape_reshape.6
  10.3 0.1 copy.20
  10.4 5.6 %all_to_all.38 = f32[2,64,4,512]{3,2,1,0:T(4,128)S(1)} all-to-all(f32[2,64,4,512]{3,2,1,0:T(4,128)S(1)} %bitcast.21), channel_id=1, replica_groups=mesh['grp'=4,'dev_0'=4,'dev_1'=4,'dev_2'=2] {'dev_2'}, dimensions={0} | all-to-all | bytes 2097152 | tf_op jit(solution)/shard_map/all_to_all | solution.py:21
  15.9 0.4 reduce_sum.18
  16.4 23.3 %all_to_all.39 = f32[64,4,512]{2,1,0:T(4,128)S(1)} all-to-all(f32[64,4,512]{2,1,0:T(4,128)S(1)} %reduce_sum.18), channel_id=1, replica_groups=mesh['grp'=4,'dev_0'=4,'dev_1'=4,'dev_2'=2] {'grp','dev_0','dev_1'}, dimensions={0} | all-to-all | bytes 1048576 | tf_op jit(solution)/shard_map/all_to_all | solution.py:29
  39.7 0.1 reduce_sum.19
  39.8 0.1 broadcast_in_dim.4
  39.9 15.5 %all_to_all.40 = f32[64,4,512]{2,1,0:T(4,128)S(1)} all-to-all(f32[64,4,512]{2,1,0:T(4,128)S(1)} %broadcast_in_dim.4), channel_id=1, replica_groups=mesh['grp'=4,'dev_0'=4,'dev_1'=4,'dev_2'=2] {'grp','dev_0','dev_1'}, dimensions={0} | all-to-all | bytes 1048576 | tf_op jit(solution)/shard_map/all_to_all | solution.py:42
  55.4 0.1 broadcast_in_dim.5
  55.5 7.4 %all_to_all.41 = f32[2,64,4,512]{3,2,1,0:T(4,128)S(1)} all-to-all(f32[2,64,4,512]{3,2,1,0:T(4,128)S(1)} %broadcast_in_dim.5), channel_id=1, replica_groups=mesh['grp'=4,'dev_0'=4,'dev_1'=4,'dev_2'=2] {'dev_2'}, dimensions={0} | all-to-all | bytes 2097152 | tf_op jit(solution)/shard_map/all_to_all | solution.py:42
  63.0 0.1 copy.15
  63.1 1.3 reshape_reshape.7.gram_ref
  64.5 47.5 %subspace.1 = f32[512,256]{1,0:T(8,128)} custom-call(f32[512,512]{1,0:T(8,128)} %reshape_reshape.7.gram_ref, f32[512,256]{1,0:T(8,128)} %start_ref.1), custom_call_target="tpu_custom_call" | custom-call | tf_op jit(solution)/shard_map/subspace/pallas_call | solution.py:155
  112.0 5.8 %convolution_bitcast_fusion = f32[64,32,256]{2,0,1:T(8,128)S(1)} fusion(f32[32,64,512]{2,1,0:T(8,128)} %param.2, f32[512,256]{1,0:T(8,128)} %subspace.1), kind=kOutput, calls=%fused_computation | convolution fusion | flops 3221225472 | bytes 6815744 | tf_op jit(solution)/shard_map/abk,kr->bar/dot_general | solution.py:178
  117.8 1.2 copy.16
  119.0 31.5 %all_to_all.42 = f32[64,32,256]{2,1,0:T(8,128)S(1)} all-to-all(f32[64,32,256]{2,1,0:T(8,128)S(1)} %copy.16), channel_id=1, replica_groups=mesh['grp'=4,'dev_0'=4,'dev_1'=4,'dev_2'=2] {'dev_0','dev_1','dev_2'}, dimensions={0} | all-to-all | bytes 4194304 | tf_op jit(solution)/shard_map/all_to_all | solution.py:179
  150.5 1.5 copy.17

commit v2 on v1

--- a/solution.py
+++ b/solution.py
@@ -1,3 +1,5 @@
+import functools
+
 import jax
 import jax.numpy as jnp
 from jax import lax
@@ -9,59 +11,7 @@
 ITERS = 4
 DEV = ("dev_0", "dev_1", "dev_2")
 GRP_DEV = ("grp", "dev_0", "dev_1", "dev_2")
-
-
-def in_blocks(shard, dim, peers):
-    before, after = (shard.shape[:dim], shard.shape[dim + 1 :])
-    return jnp.moveaxis(shard.reshape(*before, peers, -1, *after), dim, 0)
-
-
-def summed_on_arrival(shard, axis, dim):
-    peers = lax.axis_size(axis)
-    blocks = lax.all_to_all(in_blocks(shard, dim, peers), axis, 0, 0, tiled=True)
-    return jnp.sum(blocks, axis=0)
-
-
-def sum_by_axis(shard, axes, dim):
-    far, near = axes
-    blocks = in_blocks(shard, dim, lax.axis_size(far))
-    nearer = summed_on_arrival(blocks, near, dim + 1)
-    arrived = lax.all_to_all(nearer, far, split_axis=0, concat_axis=0, tiled=True)
-    return arrived.sum(axis=0)
-
-
-def rows_for(lines, peers):
-    spare = -lines.shape[0] % peers
-    if not spare:
-        return lines
-    return jnp.concatenate([lines, jnp.zeros((spare, *lines.shape[1:]), lines.dtype)])
-
-
-def copy_for_each(shard, axis):
-    peers = lax.axis_size(axis)
-    return lax.all_to_all(
-        jnp.broadcast_to(shard[None], (peers, *shard.shape)), axis, 0, 0, tiled=True
-    )
-
-
-def laid_out(blocks, dim):
-    shape = list(blocks.shape[1:])
-    shape[dim] *= blocks.shape[0]
-    return jnp.moveaxis(blocks, 0, dim).reshape(shape)
-
-
-def gather_axes(shard, axes, dim):
-    far, near = axes
-    initial = copy_for_each(shard, far)
-    blocks = jnp.swapaxes(copy_for_each(initial, near), 0, 1)
-    return laid_out(blocks.reshape(-1, *shard.shape), dim)
-
-
-def total_of(shard, axes):
-    lines = shard.reshape(-1, shard.shape[-1])
-    own = sum_by_axis(rows_for(lines, lax.axis_size(axes[0]) * lax.axis_size(axes[1])), axes, 0)
-    whole = gather_axes(own, axes, 0)
-    return whole[: len(lines)].reshape(shard.shape)
+AXES = GRP_DEV
 
 
 HIGHEST = lax.Precision.HIGHEST
@@ -167,13 +117,153 @@
     )(gram, start)
 
 
+MESH = pl.DeviceIdType.MESH
+TILE = 128
+CHUNKS = 4
+
+
+def halves_of(x):
+    high = x.astype(jnp.bfloat16)
+    return high, (x - high.astype(jnp.float32)).astype(jnp.bfloat16)
+
+
+def sum_gram(side, scale, slab_ref, gram_ref, slab, acc, part, pair, mine, arrived, line, whole, load_sem, send_sem, recv_sem):
+    y, x, z, core = (lax.axis_index(name) for name in AXES)
+    columns = gram_ref.shape[0]
+    tiles = columns // TILE
+    blocks = [(i, j) for i in range(tiles) for j in range(i, tiles)]
+    half = len(blocks) // 2
+    place = x * side + z
+    plane = [(dx, dz) for dx in range(side) for dz in range(side) if dx or dz]
+
+    def at(dy, dx, dz, dc):
+        return {
+            "grp": lax.rem(y + dy, side),
+            "dev_0": lax.rem(x + dx, side),
+            "dev_1": lax.rem(z + dz, side),
+            "dev_2": lax.rem(core + dc, 2),
+        }
+
+    depth = slab_ref.shape[0] // CHUNKS
+    loads = [
+        pltpu.make_async_copy(slab_ref.at[pl.ds(n * depth, depth)], slab.at[n], load_sem.at[n]) for n in range(CHUNKS)
+    ]
+    for load in loads:
+        load.start()
+    barrier = pltpu.get_barrier_semaphore()
+    others = [(0, dx, dz, dc) for dx in range(side) for dz in range(side) for dc in range(2) if dx or dz or dc]
+    others += [(dy, 0, 0, 0) for dy in range(1, side)]
+    for offsets in others:
+        pl.semaphore_signal(barrier, inc=1, device_id=at(*offsets), device_id_type=MESH)
+
+    for n in range(CHUNKS):
+        loads[n].wait()
+        high, low = halves_of(slab[n].reshape(-1, columns))
+        left = jnp.concatenate([high, high, low], axis=0)
+        right = jnp.concatenate([high, low, high], axis=0)
+        for lo in range(0, columns, 256):
+            new = lax.dot_general(
+                left[:, : lo + 256], right[:, lo : lo + 256], (((0,), (0,)), ((), ())), preferred_element_type=jnp.float32
+            )
+            if n:
+                new = acc[: lo + 256, lo : lo + 256] + new
+            acc[: lo + 256, lo : lo + 256] = new
+    for n, (i, j) in enumerate(blocks):
+        part[n] = acc[i * TILE : (i + 1) * TILE, j * TILE : (j + 1) * TILE] * scale
+    pl.semaphore_wait(barrier, len(others))
+
+    def send(src, dst, slot, offsets):
+        return pltpu.make_async_remote_copy(
+            src_ref=src,
+            dst_ref=dst,
+            send_sem=send_sem.at[slot],
+            recv_sem=recv_sem.at[slot],
+            device_id=at(*offsets),
+            device_id_type=MESH,
+        )
+
+    swap = send(part.at[pl.ds((1 - core) * half, half)], pair, 0, (0, 0, 0, 1))
+    swap.start()
+    swap.wait()
+    mine[...] = part[pl.ds(core * half, half)] + pair[...]
+
+    def rows_of(index):
+        return pl.ds(pl.multiple_of(index * 8, 8), 8)
+
+    copies = []
+    for n, (dx, dz) in enumerate(plane):
+        target = lax.rem(x + dx, side) * side + lax.rem(z + dz, side)
+        copies.append(send(mine.at[:, rows_of(target), :], arrived.at[n], 1 + n, (0, dx, dz, 0)))
+        copies[-1].start()
+    total = mine[:, rows_of(place), :]
+    for n, copy in enumerate(copies):
+        copy.wait_recv()
+        total = total + arrived[n]
+    line[y] = total
+    for copy in copies:
+        copy.wait_send()
+
+    base = 1 + len(plane)
+    copies = []
+    for dy in range(1, side):
+        copies.append(send(line.at[y], line.at[y], base + dy - 1, (dy, 0, 0, 0)))
+        copies[-1].start()
+    for copy in copies:
+        copy.wait()
+    total = line[0]
+    for k in range(1, side):
+        total = total + line[k]
+    own = whole.at[pl.ds(core * half, half), rows_of(place), :]
+    own[...] = total
+
+    base += side - 1
+    copies = []
+    for n, offsets in enumerate(others[: 2 * side * side - 1]):
+        copies.append(send(own, own, base + n, offsets))
+        copies[-1].start()
+    for copy in copies:
+        copy.wait()
+    for n, (i, j) in enumerate(blocks):
+        block = whole[n]
+        gram_ref[i * TILE : (i + 1) * TILE, j * TILE : (j + 1) * TILE] = block
+        if i != j:
+            gram_ref[j * TILE : (j + 1) * TILE, i * TILE : (i + 1) * TILE] = block.T
+
+
+def summed_gram(slab, scale):
+    columns = slab.shape[-1]
+    side = lax.axis_size("grp")
+    tiles = columns // TILE
+    half = tiles * (tiles + 1) // 4
+    slots = 3 * side * side + side - 2
+    return pl.pallas_call(
+        functools.partial(sum_gram, side, scale),
+        out_shape=jax.ShapeDtypeStruct((columns, columns), jnp.float32),
+        in_specs=[pl.BlockSpec(memory_space=pl.ANY)],
+        out_specs=pl.BlockSpec(memory_space=pltpu.VMEM),
+        scratch_shapes=[
+            pltpu.VMEM((CHUNKS, slab.shape[0] // CHUNKS, *slab.shape[1:]), jnp.float32),
+            pltpu.VMEM((columns, columns), jnp.float32),
+            pltpu.VMEM((2 * half, TILE, TILE), jnp.float32),
+            pltpu.VMEM((half, TILE, TILE), jnp.float32),
+            pltpu.VMEM((half, TILE, TILE), jnp.float32),
+            pltpu.VMEM((side * side - 1, half, 8, TILE), jnp.float32),
+            pltpu.VMEM((side, half, 8, TILE), jnp.float32),
+            pltpu.VMEM((2 * half, TILE, TILE), jnp.float32),
+            pltpu.SemaphoreType.DMA((CHUNKS,)),
+            pltpu.SemaphoreType.DMA((slots,)),
+            pltpu.SemaphoreType.DMA((slots,)),
+        ],
+        compiler_params=pltpu.CompilerParams(collective_id=0, has_side_effects=True),
+        name="sum_gram",
+    )(slab)
+
+
 def on_device(slab, start):
     highest = lax.Precision.HIGHEST
     a_local, points, columns = slab.shape
-    matrix = slab.reshape(a_local * points, columns)
-    scale = jnp.float32(1.0 / (a_local * points * lax.axis_size("grp") * lax.axis_size(DEV)))
-    local_gram = jnp.dot(matrix.T, matrix, precision=highest) * scale
-    gram = total_of(local_gram, (("grp", "dev_0", "dev_1"), "dev_2"))
+    scale = 1.0 / (a_local * points * lax.axis_size("grp") * lax.axis_size(DEV))
+    gram = summed_gram(slab, scale)
     basis = subspace(gram, start)
     projected = jnp.einsum("abk,kr->bar", slab, basis, precision=highest)
     regrouped = lax.all_to_all(projected, DEV, split_axis=0, concat_axis=1, tiled=True)

time: 152 us -> 125 us (0.82)
  blocking collectives: 83.3 us -> 33.2 us
  Pallas kernels: 47.5 us -> 82.3 us
  matrix products: 15.2 us -> 5.84 us
  local copies, waits for them, and re-layouts: 4.74 us -> 2.67 us
    all_to_all x4 -> x0, blocking collectives: 51.9 us -> none  [the longest x1 23.3 us: sum_by_axis(): lax.all_to_all(nearer, far, split_axis=0, concat_axis=0, tiled=True)]
    pallas_call x0 -> x1, Pallas kernels: none -> 34.7 us  [summed_gram(): pl.pallas_call(functools.partial(sum_gram, side, scale), out_shape=jax.Sh...]
    dot_general x1 -> x0, matrix products: 9.33 us -> none  [on_device(): local_gram = jnp.dot(matrix.T, matrix, precision=highest) * scale]
    another operation x3 -> x0, local copies, waits for them, and re-layouts: 1.73 us -> none  [the longest x1 1.34 us: laid_out(): return jnp.moveaxis(blocks, 0, dim).reshape(shape)]
    all_to_all x1, blocking collectives: 31.5 us -> 33.2 us  [on_device(): lax.all_to_all(projected, DEV, split_axis=0, concat_axis=1, tiled=True)]
where the time goes in v2:
time: 125 us
  Pallas kernels  82.3 us (66%)
  blocking collectives  33.2 us (27%)
  matrix products  5.84 us (5%)
  local copies, waits for them, and re-layouts  2.67 us (2%)
    pallas_call x1, Pallas kernels, subspace(): pl.pallas_call(iterate, out_shape=jax.ShapeDtypeStruct((columns, rank), j...  47.7 us
    pallas_call x1, Pallas kernels, summed_gram(): pl.pallas_call(functools.partial(sum_gram, side, scale), out_shape=jax.Sh...  34.7 us
    all_to_all x1, blocking collectives, on_device(): lax.all_to_all(projected, DEV, split_axis=0, concat_axis=1, tiled=True)  33.2 us
    dot_general x1, matrix products, on_device(): projected = jnp.einsum('abk,kr->bar', slab, basis, precision=highest)  5.84 us

profile of v2, /device:TPU:1, one launch (start us, length us, event | category | flops | bytes accessed | tf_op | source)
XLA Modules:
  0.0 124.7 jit_solution(14655312212265434822)
XLA Ops:
  0.6 34.7 %sum_gram.1.gram_ref = f32[512,512]{1,0:T(8,128)} custom-call(f32[32,64,512]{2,1,0:T(8,128)} %slab_ref.1), custom_call_target="tpu_custom_call" | custom-call | tf_op jit(solution)/shard_map/sum_gram/pallas_call | solution.py:239
  35.3 47.7 %subspace.1 = f32[512,256]{1,0:T(8,128)} custom-call(f32[512,512]{1,0:T(8,128)} %sum_gram.1.gram_ref, f32[512,256]{1,0:T(8,128)} %start_ref.1), custom_call_target="tpu_custom_call" | custom-call | tf_op jit(solution)/shard_map/subspace/pallas_call | solution.py:105
  83.0 5.8 %convolution_bitcast_fusion = f32[64,32,256]{2,0,1:T(8,128)S(1)} fusion(f32[32,64,512]{2,1,0:T(8,128)} %slab_ref.1, f32[512,256]{1,0:T(8,128)} %subspace.1), kind=kOutput, calls=%fused_computation | convolution fusion | flops 3221225472 | bytes 6815744 | tf_op jit(solution)/shard_map/abk,kr->bar/dot_general | solution.py:268
  88.8 1.2 copy.5
  90.0 33.2 %all_to_all.18 = f32[64,32,256]{2,1,0:T(8,128)S(1)} all-to-all(f32[64,32,256]{2,1,0:T(8,128)S(1)} %copy.5), channel_id=1, replica_groups=mesh['grp'=4,'dev_0'=4,'dev_1'=4,'dev_2'=2] {'dev_0','dev_1','dev_2'}, dimensions={0} | all-to-all | bytes 4194304 | tf_op jit(solution)/shard_map/all_to_all | solution.py:269
  123.2 1.5 %copy.6 = f32[2,32,32,256]{3,2,1,0:T(8,128)} copy(f32[2,32,32,256]{3,2,0,1:T(8,128)S(1)} %bitcast.10) | data formatting | bytes 4194304 | tf_op jit(solution)/shard_map/all_to_all | solution.py:269

commit v3 on v2

--- a/solution.py
+++ b/solution.py
@@ -12,6 +12,7 @@
 DEV = ("dev_0", "dev_1", "dev_2")
 GRP_DEV = ("grp", "dev_0", "dev_1", "dev_2")
 AXES = GRP_DEV
+MESH = pl.DeviceIdType.MESH
 
 
 HIGHEST = lax.Precision.HIGHEST
@@ -86,7 +87,48 @@
             v_ref[hi:, :hi] -= contract(down, v_ref[lo:hi, :hi], 1, 0)
 
 
-def iterate(gram_ref, start_ref, basis_ref, rows_ref, product_ref, m_ref, v_ref):
+def iterate(side, gram_ref, start_ref, slab_ref, basis_ref, moved_ref, rows_ref, product_ref, m_ref, v_ref, own_sem, send_sem, recv_sem):
+    x, z, core = (lax.axis_index(name) for name in DEV)
+    count = slab_ref.shape[0]
+    held = moved_ref.shape[0]
+
+    def place(x, z, core):
+        return (x * side + z) * 2 + core
+
+    def rows_here(index):
+        return pl.ds(pl.multiple_of(index * count, count), count)
+
+    peers = []
+    for dx in range(side):
+        for dz in range(side):
+            for dc in range(2):
+                if dx or dz or dc:
+                    peers.append((lax.rem(x + dx, side), lax.rem(z + dz, side), lax.rem(core + dc, 2)))
+    barrier = pltpu.get_barrier_semaphore()
+    for peer in peers:
+        pl.semaphore_signal(barrier, inc=1, device_id=dict(zip(DEV, peer)), device_id_type=MESH)
+    pl.semaphore_wait(barrier, len(peers))
+    me = place(x, z, core)
+    copies = []
+    for n, peer in enumerate(peers):
+        for i in range(held):
+            copies.append(
+                pltpu.make_async_remote_copy(
+                    src_ref=slab_ref.at[:, place(*peer) * held + i, :],
+                    dst_ref=moved_ref.at[i, rows_here(me), :],
+                    send_sem=send_sem.at[n, i],
+                    recv_sem=recv_sem.at[n, i],
+                    device_id=dict(zip(DEV, peer)),
+                    device_id_type=MESH,
+                )
+            )
+    for i in range(held):
+        copies.append(
+            pltpu.make_async_copy(slab_ref.at[:, me * held + i, :], moved_ref.at[i, rows_here(me), :], own_sem.at[i])
+        )
+    for copy in copies:
+        copy.start()
+
     rows_ref[...] = start_ref[...].T
 
     def step(_, carry):
@@ -98,26 +140,64 @@
 
     lax.fori_loop(0, ITERS, step, 0)
     basis_ref[...] = rows_ref[...].T
-
-
-def subspace(gram, start):
+    for copy in copies:
+        copy.wait()
+
+
+def subspace(gram, start, slab):
     columns, rank = start.shape
+    count, points, _ = slab.shape
+    peers = lax.axis_size(DEV)
+    held = points // peers
+    vmem = pl.BlockSpec(memory_space=pltpu.VMEM)
+    hbm = pl.BlockSpec(memory_space=pl.ANY)
     return pl.pallas_call(
-        iterate,
-        out_shape=jax.ShapeDtypeStruct((columns, rank), jnp.float32),
-        in_specs=[pl.BlockSpec(memory_space=pltpu.VMEM)] * 2,
-        out_specs=pl.BlockSpec(memory_space=pltpu.VMEM),
+        functools.partial(iterate, lax.axis_size("grp")),
+        out_shape=(
+            jax.ShapeDtypeStruct((columns, rank), jnp.float32),
+            jax.ShapeDtypeStruct((held, count * peers, columns), jnp.float32),
+        ),
+        in_specs=[vmem, vmem, hbm],
+        out_specs=(vmem, hbm),
         scratch_shapes=[
             pltpu.VMEM((rank, columns), jnp.float32),
             pltpu.VMEM((rank, columns), jnp.float32),
             pltpu.VMEM((rank, rank), jnp.float32),
             pltpu.VMEM((rank, rank), jnp.float32),
+            pltpu.SemaphoreType.DMA((held,)),
+            pltpu.SemaphoreType.DMA((peers - 1, held)),
+            pltpu.SemaphoreType.DMA((peers - 1, held)),
         ],
+        compiler_params=pltpu.CompilerParams(collective_id=1, has_side_effects=True),
         name="subspace",
-    )(gram, start)
-
-
-MESH = pl.DeviceIdType.MESH
+    )(gram, start, slab)
+
+
+def project(rows_ref, basis_ref, out_ref):
+    high, low = halves_of(rows_ref[...])
+    basis_high, basis_low = halves_of(basis_ref[...])
+    left = jnp.concatenate([high, high, low], axis=1)
+    right = jnp.concatenate([basis_high, basis_low, basis_high], axis=0)
+    out_ref[...] = lax.dot_general(left, right, (((1,), (0,)), ((), ())), preferred_element_type=jnp.float32)
+
+
+def projected_rows(moved, basis):
+    held, count, columns = moved.shape
+    rank = basis.shape[1]
+    rows = 256
+    return pl.pallas_call(
+        project,
+        out_shape=jax.ShapeDtypeStruct((held * count, rank), jnp.float32),
+        grid=(held * count // rows,),
+        in_specs=[
+            pl.BlockSpec((rows, columns), lambda n: (n, 0)),
+            pl.BlockSpec((columns, rank), lambda n: (0, 0)),
+        ],
+        out_specs=pl.BlockSpec((rows, rank), lambda n: (n, 0)),
+        name="project",
+    )(moved.reshape(held * count, columns), basis).reshape(held, count, rank)
+
+
 TILE = 128
 CHUNKS = 4
 
@@ -260,14 +340,11 @@
 
 
 def on_device(slab, start):
-    highest = lax.Precision.HIGHEST
-    a_local, points, columns = slab.shape
+    a_local, points, _ = slab.shape
     scale = 1.0 / (a_local * points * lax.axis_size("grp") * lax.axis_size(DEV))
     gram = summed_gram(slab, scale)
-    basis = subspace(gram, start)
-    projected = jnp.einsum("abk,kr->bar", slab, basis, precision=highest)
-    regrouped = lax.all_to_all(projected, DEV, split_axis=0, concat_axis=1, tiled=True)
-    return (regrouped, basis)
+    basis, moved = subspace(gram, start, slab)
+    return (projected_rows(moved, basis), basis)
 
 
 def solution(mesh):

time: 125 us -> 120 us (0.960)
  Pallas kernels: 82.3 us -> 117 us
  blocking collectives: 33.2 us -> 0 us
  matrix products: 5.84 us -> 0 us
  local copies, waits for them, and re-layouts: 2.67 us -> 0.8 us
    pallas_call x1 -> x2, Pallas kernels: 47.7 us -> 82.8 us  [the longest x1 75.1 us: subspace(): pl.pallas_call(functools.partial(iterate, lax.axis_size('grp')), out_shap...]
    all_to_all x1 -> x0, blocking collectives: 33.2 us -> none  [on_device(): lax.all_to_all(projected, DEV, split_axis=0, concat_axis=1, tiled=True)]
    dot_general x1 -> x0, matrix products: 5.84 us -> none  [on_device(): projected = jnp.einsum('abk,kr->bar', slab, basis, precision=highest)]
    all_to_all x1 -> x0, local copies, waits for them, and re-layouts: 1.46 us -> none  [on_device(): lax.all_to_all(projected, DEV, split_axis=0, concat_axis=1, tiled=True)]
where the time goes in v3:
time: 120 us; the launch traced here: 119 us
  Pallas kernels  117 us (98%)
    pallas_call x1, Pallas kernels, subspace(): pl.pallas_call(functools.partial(iterate, lax.axis_size('grp')), out_shap...  75.1 us
    pallas_call x1, Pallas kernels, summed_gram(): pl.pallas_call(functools.partial(sum_gram, side, scale), out_shape=jax.Sh...  34.6 us
    pallas_call x1, Pallas kernels, projected_rows(): pl.pallas_call(project, out_shape=jax.ShapeDtypeStruct((held * count, ran...  7.67 us

profile of v3, /device:TPU:1, one launch (start us, length us, event | category | flops | bytes accessed | tf_op | source)
XLA Modules:
  0.0 118.9 jit_solution(12314135584963459231)
XLA Ops:
  0.6 34.6 %sum_gram.1.gram_ref = f32[512,512]{1,0:T(8,128)} custom-call(f32[32,64,512]{2,1,0:T(8,128)} %slab_ref.3), custom_call_target="tpu_custom_call" | custom-call | tf_op jit(solution)/shard_map/sum_gram/pallas_call | solution.py:319
  35.3 75.1 %subspace.1 = (f32[512,256]{1,0:T(8,128)}, f32[2,1024,512]{2,1,0:T(8,128)}) custom-call(f32[512,512]{1,0:T(8,128)} %sum_gram.1.gram_ref, f32[512,256]{1,0:T(8,128)} %start_ref.1, f32[32,64,512]{2,1,0:T(8,128)} %slab_ref.3), custom_call_target="tpu_custom_call" | custom-call | tf_op jit(solution)/shard_map/subspace/pallas_call | solution.py:154
  110.4 0.0 copy-start
  110.4 7.7 %project.1 = f32[2048,256]{1,0:T(8,128)} custom-call(f32[2048,512]{1,0:T(8,128)} %bitcast.2, f32[512,256]{1,0:T(8,128)} %get-tuple-element.9.basis_ref), custom_call_target="tpu_custom_call" | custom-call | tf_op jit(solution)/shard_map/project/pallas_call | solution.py:188
  118.1 0.0 copy-done
  118.1 0.8 copy.5
Async XLA Ops:
  110.4 7.7 %copy-start = (f32[512,256]{1,0:T(8,128)S(1)}, f32[512,256]{1,0:T(8,128)}, u32[]{:S(2)}) copy-start(f32[512,256]{1,0:T(8,128)} %get-tuple-element.9.basis_ref) | copy-start | bytes 1572868

commit v4 on v3

--- a/solution.py
+++ b/solution.py
@@ -17,6 +17,7 @@
 
 HIGHEST = lax.Precision.HIGHEST
 BLOCK = 64
+PANEL = 16
 
 
 def contract(a, b, dim_a, dim_b):
@@ -25,7 +26,7 @@
     )
 
 
-def inverse_factor(block):
+def inverse_factor(block, spread_ref):
     size = block.shape[0]
     diagonal = lax.broadcasted_iota(jnp.int32, (size, size), 0) == lax.broadcasted_iota(jnp.int32, (size, size), 1)
     both = jnp.concatenate([block, diagonal.astype(jnp.float32)], axis=1)
@@ -33,61 +34,89 @@
     count = size // 8
     tiles = [both[8 * t : 8 * t + 8, :] for t in range(count)]
     row_of = lax.broadcasted_iota(jnp.int32, wide, 0)
-    for t in range(count):
-        cols = [[jnp.broadcast_to(tiles[u][:, 8 * t + c : 8 * t + c + 1], wide) for u in range(t, count)] for c in range(8)]
-        rows = [jnp.broadcast_to(tiles[t][i : i + 1, :], wide) for i in range(8)]
-        a = [
-            [
-                jnp.broadcast_to(jnp.sum(jnp.where(row_of == i, cols[c][0], 0.0), axis=0, keepdims=True), wide)
-                if i >= c
-                else None
-                for c in range(8)
-            ]
-            for i in range(8)
+
+    def over_rows(row):
+        return jnp.broadcast_to(row, wide)
+
+    for first in range(0, count, PANEL // 8):
+        after = first + PANEL // 8
+        cols = [
+            [jnp.broadcast_to(tiles[u][:, 8 * first + c : 8 * first + c + 1], wide) for u in range(first, count)]
+            for c in range(PANEL)
         ]
-        unit = [[None] * 8 for _ in range(8)]
-        scaled = []
-        for c in range(8):
-            inverse = 1.0 / a[c][c]
-            for i in range(c + 1, 8):
-                unit[i][c] = a[i][c] * inverse
-            for k in range(c + 1, 8):
-                for i in range(k, 8):
-                    a[i][k] = a[i][k] - unit[i][c] * a[k][c]
-            for i in range(c + 1, 8):
-                rows[i] = rows[i] - unit[i][c] * rows[c]
+        for t in range(first, after):
+            spread_ref[PANEL + t - first] = tiles[t]
+        spread_ref[0] = cols[0][0]
+        for t in range(1, PANEL // 8):
+            spread_ref[PANEL + PANEL // 8 + t - 1] = cols[0][t]
+        rows = [over_rows(spread_ref[PANEL + i // 8, i % 8 : i % 8 + 1, :]) for i in range(PANEL)]
+        pivots, scaled = [], []
+        for c in range(PANEL):
+            def at(i):
+                if c == 0:
+                    slot = 0 if i < 8 else PANEL + PANEL // 8 + i // 8 - 1
+                    return over_rows(spread_ref[slot, i % 8 : i % 8 + 1, :])
+                return over_rows(cols[c][i // 8][i % 8 : i % 8 + 1, :])
+
+            pivots.append(at(c))
+            inverse = 1.0 / pivots[c]
+            for k in range(c + 1, PANEL):
+                factor = at(k) * inverse
+                for u in range(k // 8, count - first):
+                    cols[k][u] = cols[k][u] - factor * cols[c][u]
+                rows[k] = rows[k] - factor * rows[c]
             scaled.append(rows[c] * inverse)
-        for u in range(t + 1, count):
-            col = [cols[c][u - t] for c in range(8)]
-            for c in range(8):
-                for k in range(c + 1, 8):
-                    col[k] = col[k] - unit[k][c] * col[c]
-            change = col[0] * scaled[0]
-            for c in range(1, 8):
-                change = change + col[c] * scaled[c]
+        for u in range(after, count):
+            change = cols[0][u - first] * scaled[0]
+            for c in range(1, PANEL):
+                change = change + cols[c][u - first] * scaled[c]
             tiles[u] = tiles[u] - change
-        for c in range(8):
-            tiles[t] = jnp.where(row_of == c, rows[c] * lax.rsqrt(a[c][c]), tiles[t])
+        for c in range(PANEL):
+            t = first + c // 8
+            tiles[t] = jnp.where(row_of == c % 8, rows[c] * lax.rsqrt(pivots[c]), tiles[t])
     return jnp.concatenate(tiles, axis=0)[:, size:]
 
 
-def inverse_cholesky(m_ref, v_ref):
+def inverse_cholesky(m_ref, v_ref, spread_ref):
     size = m_ref.shape[0]
     v_ref[...] = jnp.zeros_like(v_ref)
+    corner = m_ref[:BLOCK, :BLOCK]
     for lo in range(0, size, BLOCK):
         hi = lo + BLOCK
-        inner = inverse_factor(m_ref[lo:hi, lo:hi])
+        end = min(hi + BLOCK, size)
+        inner = inverse_factor(corner, spread_ref)
+        if hi < size:
+            across = contract(inner, m_ref[lo:hi, hi:end], 1, 0)
+            down = contract(m_ref[hi:end, lo:hi], inner, 1, 1)
+            corner = m_ref[hi:end, hi:end] - contract(down, across, 1, 0)
         if lo:
             v_ref[lo:hi, :lo] = contract(inner, v_ref[lo:hi, :lo], 1, 0)
         v_ref[lo:hi, lo:hi] = inner
+        if end < size:
+            far_across = contract(inner, m_ref[lo:hi, end:], 1, 0)
+            far_down = contract(m_ref[end:, lo:hi], inner, 1, 1)
+            m_ref[hi:end, end:] -= contract(down, far_across, 1, 0)
+            m_ref[end:, hi:end] -= contract(far_down, across, 1, 0)
+            m_ref[end:, end:] -= contract(far_down, far_across, 1, 0)
+            v_ref[end:, :hi] -= contract(far_down, v_ref[lo:hi, :hi], 1, 0)
         if hi < size:
-            across = contract(inner, m_ref[lo:hi, hi:], 1, 0)
-            down = contract(m_ref[hi:, lo:hi], inner, 1, 1)
-            m_ref[hi:, hi:] -= contract(down, across, 1, 0)
-            v_ref[hi:, :hi] -= contract(down, v_ref[lo:hi, :hi], 1, 0)
-
-
-def iterate(side, gram_ref, start_ref, slab_ref, basis_ref, moved_ref, rows_ref, product_ref, m_ref, v_ref, own_sem, send_sem, recv_sem):
+            v_ref[hi:end, :hi] -= contract(down, v_ref[lo:hi, :hi], 1, 0)
+
+
+def far_first(side):
+    def hops(offset):
+        return sum(min(step, side - step) for step in offset)
+
+    order = []
+    for dx, dz in sorted(((dx, dz) for dx in range(side) for dz in range(side)), key=lambda o: (-hops(o), o)):
+        back_x, back_z = (side - dx) % side, (side - dz) % side
+        for offset in ((dx, dz), (back_x, back_z), (dz, back_x), (back_z, dx)):
+            if offset not in order and any(offset):
+                order.append(offset)
+    return order
+
+
+def iterate(side, gram_ref, start_ref, slab_ref, basis_ref, moved_ref, rows_ref, product_ref, m_ref, v_ref, spread_ref, own_sem, send_sem, recv_sem):
     x, z, core = (lax.axis_index(name) for name in DEV)
     count = slab_ref.shape[0]
     held = moved_ref.shape[0]
@@ -98,12 +127,12 @@
     def rows_here(index):
         return pl.ds(pl.multiple_of(index * count, count), count)
 
-    peers = []
-    for dx in range(side):
-        for dz in range(side):
-            for dc in range(2):
-                if dx or dz or dc:
-                    peers.append((lax.rem(x + dx, side), lax.rem(z + dz, side), lax.rem(core + dc, 2)))
+    peers = [(x, z, 1 - core)]
+    for dx, dz in far_first(side):
+        for dc in range(2):
+            step_x = dx + core * ((side - dx) % side - dx)
+            step_z = dz + core * ((side - dz) % side - dz)
+            peers.append((lax.rem(x + step_x, side), lax.rem(z + step_z, side), lax.rem(core + dc, 2)))
     barrier = pltpu.get_barrier_semaphore()
     for peer in peers:
         pl.semaphore_signal(barrier, inc=1, device_id=dict(zip(DEV, peer)), device_id_type=MESH)
@@ -134,7 +163,7 @@
     def step(_, carry):
         product_ref[...] = contract(rows_ref[...], gram_ref[...], 1, 0)
         m_ref[...] = contract(product_ref[...], product_ref[...], 1, 1)
-        inverse_cholesky(m_ref, v_ref)
+        inverse_cholesky(m_ref, v_ref, spread_ref)
         rows_ref[...] = contract(v_ref[...], product_ref[...], 1, 0)
         return carry
 
@@ -164,6 +193,7 @@
             pltpu.VMEM((rank, columns), jnp.float32),
             pltpu.VMEM((rank, rank), jnp.float32),
             pltpu.VMEM((rank, rank), jnp.float32),
+            pltpu.VMEM((PANEL + PANEL // 4, 8, 2 * BLOCK), jnp.float32),
             pltpu.SemaphoreType.DMA((held,)),
             pltpu.SemaphoreType.DMA((peers - 1, held)),
             pltpu.SemaphoreType.DMA((peers - 1, held)),

time: 120 us -> 103 us (0.86)
  Pallas kernels: 117 us -> 102 us
    pallas_call x1, Pallas kernels: 75.1 us -> 59.3 us  [subspace(): pl.pallas_call(functools.partial(iterate, lax.axis_size('grp')), out_shap...]
where the time goes in v4:
time: 103 us
  Pallas kernels  102 us (99%)
    pallas_call x1, Pallas kernels, subspace(): pl.pallas_call(functools.partial(iterate, lax.axis_size('grp')), out_shap...  59.3 us
    pallas_call x1, Pallas kernels, summed_gram(): pl.pallas_call(functools.partial(sum_gram, side, scale), out_shape=jax.Sh...  34.6 us
    pallas_call x1, Pallas kernels, projected_rows(): pl.pallas_call(project, out_shape=jax.ShapeDtypeStruct((held * count, ran...  7.66 us

profile of v4, /device:TPU:1, one launch (start us, length us, event | category | flops | bytes accessed | tf_op | source)
XLA Modules:
  0.0 103.0 jit_solution(7372309479530736950)
XLA Ops:
  0.6 34.6 %sum_gram.1.gram_ref = f32[512,512]{1,0:T(8,128)} custom-call(f32[32,64,512]{2,1,0:T(8,128)} %slab_ref.3), custom_call_target="tpu_custom_call" | custom-call | tf_op jit(solution)/shard_map/sum_gram/pallas_call | solution.py:349
  35.3 59.3 %subspace.1 = (f32[512,256]{1,0:T(8,128)}, f32[2,1024,512]{2,1,0:T(8,128)}) custom-call(f32[512,512]{1,0:T(8,128)} %sum_gram.1.gram_ref, f32[512,256]{1,0:T(8,128)} %start_ref.1, f32[32,64,512]{2,1,0:T(8,128)} %slab_ref.3), custom_call_target="tpu_custom_call" | custom-call | tf_op jit(solution)/shard_map/subspace/pallas_call | solution.py:183
  94.6 0.0 copy-start
  94.6 7.7 %project.1 = f32[2048,256]{1,0:T(8,128)} custom-call(f32[2048,512]{1,0:T(8,128)} %bitcast.2, f32[512,256]{1,0:T(8,128)} %get-tuple-element.9.basis_ref), custom_call_target="tpu_custom_call" | custom-call | tf_op jit(solution)/shard_map/project/pallas_call | solution.py:218
  102.2 0.0 copy-done
  102.2 0.8 copy.5
Async XLA Ops:
  94.6 7.7 %copy-start = (f32[512,256]{1,0:T(8,128)S(1)}, f32[512,256]{1,0:T(8,128)}, u32[]{:S(2)}) copy-start(f32[512,256]{1,0:T(8,128)} %get-tuple-element.9.basis_ref) | copy-start | bytes 1572868

commit v5 on v4

v5 whole, which is shorter than its diff:
```python
import functools

import jax
import jax.numpy as jnp
from jax import lax
from jax.experimental import pallas as pl
from jax.experimental.pallas import tpu as pltpu
from jax.sharding import Mesh
from jax.sharding import PartitionSpec as P

ITERS = 4
DEV = ("dev_0", "dev_1", "dev_2")
AXES = ("grp", *DEV)
MESH = pl.DeviceIdType.MESH
HIGHEST = lax.Precision.HIGHEST
BLOCK = 64
PANEL = 16
TILE = 128
CHUNKS = 4
STRIPE = 256
EARLY = 9
MIDDLE = 2


def contract(a, b, dim_a, dim_b):
    return lax.dot_general(
        a, b, (((dim_a,), (dim_b,)), ((), ())), precision=HIGHEST, preferred_element_type=jnp.float32
    )


def inverse_factor(block, spread_ref):
    size = block.shape[0]
    diagonal = lax.broadcasted_iota(jnp.int32, (size, size), 0) == lax.broadcasted_iota(jnp.int32, (size, size), 1)
    both = jnp.concatenate([block, diagonal.astype(jnp.float32)], axis=1)
    wide = (8, 2 * size)
    count = size // 8
    tiles = [both[8 * t : 8 * t + 8, :] for t in range(count)]
    row_of = lax.broadcasted_iota(jnp.int32, wide, 0)

    def over_rows(row):
        return jnp.broadcast_to(row, wide)

    for first in range(0, count, PANEL // 8):
        after = first + PANEL // 8
        cols = [
            [jnp.broadcast_to(tiles[u][:, 8 * first + c : 8 * first + c + 1], wide) for u in range(first, count)]
            for c in range(PANEL)
        ]
        for t in range(first, after):
            spread_ref[PANEL + t - first] = tiles[t]
        spread_ref[0] = cols[0][0]
        for t in range(1, PANEL // 8):
            spread_ref[PANEL + PANEL // 8 + t - 1] = cols[0][t]
        rows = [over_rows(spread_ref[PANEL + i // 8, i % 8 : i % 8 + 1, :]) for i in range(PANEL)]
        pivots, scaled = [], []
        for c in range(PANEL):
            def at(i):
                if c == 0:
                    slot = 0 if i < 8 else PANEL + PANEL // 8 + i // 8 - 1
                    return over_rows(spread_ref[slot, i % 8 : i % 8 + 1, :])
                return over_rows(cols[c][i // 8][i % 8 : i % 8 + 1, :])

            pivots.append(at(c))
            inverse = 1.0 / pivots[c]
            for k in range(c + 1, PANEL):
                factor = at(k) * inverse
                for u in range(k // 8, count - first):
                    cols[k][u] = cols[k][u] - factor * cols[c][u]
                rows[k] = rows[k] - factor * rows[c]
            scaled.append(rows[c] * inverse)
        for u in range(after, count):
            change = cols[0][u - first] * scaled[0]
            for c in range(1, PANEL):
                change = change + cols[c][u - first] * scaled[c]
            tiles[u] = tiles[u] - change
        for c in range(PANEL):
            t = first + c // 8
            tiles[t] = jnp.where(row_of == c % 8, rows[c] * lax.rsqrt(pivots[c]), tiles[t])
    return jnp.concatenate(tiles, axis=0)[:, size:]


def inverse_cholesky(m_ref, v_ref, spread_ref):
    size = m_ref.shape[0]
    v_ref[...] = jnp.zeros_like(v_ref)
    corner = m_ref[:BLOCK, :BLOCK]
    for lo in range(0, size, BLOCK):
        hi = lo + BLOCK
        end = min(hi + BLOCK, size)
        inner = inverse_factor(corner, spread_ref)
        if hi < size:
            across = contract(inner, m_ref[lo:hi, hi:end], 1, 0)
            down = contract(m_ref[hi:end, lo:hi], inner, 1, 1)
            corner = m_ref[hi:end, hi:end] - contract(down, across, 1, 0)
        if lo:
            v_ref[lo:hi, :lo] = contract(inner, v_ref[lo:hi, :lo], 1, 0)
        v_ref[lo:hi, lo:hi] = inner
        if end < size:
            far_across = contract(inner, m_ref[lo:hi, end:], 1, 0)
            far_down = contract(m_ref[end:, lo:hi], inner, 1, 1)
            m_ref[hi:end, end:] -= contract(down, far_across, 1, 0)
            m_ref[end:, hi:end] -= contract(far_down, across, 1, 0)
            m_ref[end:, end:] -= contract(far_down, far_across, 1, 0)
            v_ref[end:, :hi] -= contract(far_down, v_ref[lo:hi, :hi], 1, 0)
        if hi < size:
            v_ref[hi:end, :hi] -= contract(down, v_ref[lo:hi, :hi], 1, 0)


def far_first(side):
    def hops(offset):
        return sum(min(step, side - step) for step in offset)

    order = []
    for dx, dz in sorted(((dx, dz) for dx in range(side) for dz in range(side)), key=lambda o: (-hops(o), o)):
        back_x, back_z = (side - dx) % side, (side - dz) % side
        for offset in ((dx, dz), (back_x, back_z), (dz, back_x), (back_z, dx)):
            if offset not in order and any(offset):
                order.append(offset)
    return order


def halves_of(x):
    high = x.astype(jnp.bfloat16)
    return high, (x - high.astype(jnp.float32)).astype(jnp.bfloat16)


def three_products(x, across):
    high, low = halves_of(x)
    return jnp.concatenate([high, low, high] if across else [high, high, low], axis=1)


def truncate(
    side,
    scale,
    slab_ref,
    start_ref,
    out_ref,
    basis_ref,
    slab,
    acc,
    part,
    pair,
    mine,
    arrived,
    line,
    whole,
    rows_ref,
    product_ref,
    m_ref,
    v_ref,
    spread_ref,
    moved,
    staged,
    load_sem,
    store_sem,
    own_sem,
    sum_send,
    sum_recv,
    row_send,
    row_recv,
):
    y, x, z, core = (lax.axis_index(name) for name in AXES)
    columns = acc.shape[0]
    tiles = columns // TILE
    blocks = [(i, j) for i in range(tiles) for j in range(i, tiles)]
    half = len(blocks) // 2
    count = slab_ref.shape[0]
    held = moved.shape[0]
    depth = count // CHUNKS

    loads = [
        pltpu.make_async_copy(slab_ref.at[pl.ds(n * depth, depth)], slab.at[n], load_sem.at[n]) for n in range(CHUNKS)
    ]
    for load in loads:
        load.start()

    def chip(offset):
        step_x, step_z = (step + core * ((side - step) % side - step) for step in offset)
        return lax.rem(x + step_x, side), lax.rem(z + step_z, side)

    plane = [chip(offset) for offset in far_first(side)]
    partner = (y, x, z, 1 - core)
    near = [(y, *to, core) for to in plane]
    peers = [(y, *to, c) for to in plane for c in (core, 1 - core)] + [partner]
    above = [(lax.rem(y + dy, side), x, z, core) for dy in range(1, side)]

    barrier = pltpu.get_barrier_semaphore()
    for to in peers + above:
        pl.semaphore_signal(barrier, inc=1, device_id=dict(zip(AXES, to)), device_id_type=MESH)

    def rows_of(index, size):
        return pl.ds(pl.multiple_of(index * size, size), size)

    def number(to):
        return (to[1] * side + to[2]) * 2 + to[3]

    me = number((y, x, z, core))
    place = x * side + z
    exchange = [
        [
            pltpu.make_async_remote_copy(
                src_ref=slab_ref.at[:, number(to) * held + i, :],
                dst_ref=moved.at[i, rows_of(me, count), :],
                send_sem=row_send.at[n, i],
                recv_sem=row_recv.at[n, i],
                device_id=dict(zip(AXES, to)),
                device_id_type=MESH,
            )
            for i in range(held)
        ]
        for n, to in enumerate(peers)
    ]
    kept = [
        pltpu.make_async_copy(slab_ref.at[:, me * held + i, :], moved.at[i, rows_of(me, count), :], own_sem.at[i])
        for i in range(held)
    ]

    def start(copies):
        for copy in copies:
            copy.start()

    for n in range(CHUNKS):
        if n == CHUNKS // 2:
            pl.semaphore_wait(barrier, len(peers + above))
            start(kept)
            for copies in exchange[len(peers) - EARLY :]:
                start(copies)
        loads[n].wait()
        high, low = halves_of(slab[n].reshape(-1, columns))
        left = jnp.concatenate([high, high, low], axis=0)
        right = jnp.concatenate([high, low, high], axis=0)
        for lo in range(0, columns, 256):
            new = lax.dot_general(
                left[:, : lo + 256], right[:, lo : lo + 256], (((0,), (0,)), ((), ())), preferred_element_type=jnp.float32
            )
            if n:
                new = acc[: lo + 256, lo : lo + 256] + new
            acc[: lo + 256, lo : lo + 256] = new
    for n, (i, j) in enumerate(blocks):
        part[n] = acc[i * TILE : (i + 1) * TILE, j * TILE : (j + 1) * TILE] * scale

    slots = iter(range(sum_send.shape[0]))

    def send(src, dst, to):
        slot = next(slots)
        copy = pltpu.make_async_remote_copy(
            src_ref=src,
            dst_ref=dst,
            send_sem=sum_send.at[slot],
            recv_sem=sum_recv.at[slot],
            device_id=dict(zip(AXES, to)),
            device_id_type=MESH,
        )
        copy.start()
        return copy

    send(part.at[pl.ds((1 - core) * half, half)], pair, partner).wait()
    own_half = pl.ds(core * half, half)
    mine[...] = part[own_half] + pair[...]

    copies = [
        send(mine.at[:, rows_of(to[1] * side + to[2], 8), :], arrived.at[n], to) for n, to in enumerate(near)
    ]
    total = mine[:, rows_of(place, 8), :]
    for n, copy in enumerate(copies):
        copy.wait_recv()
        total = total + arrived[n]
    line[y] = total
    for copy in copies:
        copy.wait_send()

    copies = [send(line.at[y], line.at[y], to) for to in above]
    for group in exchange[:MIDDLE]:
        start(group)
    for copy in copies:
        copy.wait()
    total = line[0]
    for k in range(1, side):
        total = total + line[k]
    own = whole.at[own_half, rows_of(place, 8), :]
    own[...] = total

    copies = [send(own, own, to) for to in near]
    passed = [send(own, own, partner)]
    for offset, copy in zip(far_first(side), copies):
        copy.wait_recv()
        back = chip(tuple((side - step) % side for step in offset))
        piece = whole.at[own_half, rows_of(back[0] * side + back[1], 8), :]
        passed.append(send(piece, piece, partner))
    for copy in copies:
        copy.wait_send()
    for copy in passed:
        copy.wait()
    for group in exchange[MIDDLE : len(peers) - EARLY]:
        start(group)

    for n, (i, j) in enumerate(blocks):
        block = whole[n]
        acc[i * TILE : (i + 1) * TILE, j * TILE : (j + 1) * TILE] = block
        if i != j:
            acc[j * TILE : (j + 1) * TILE, i * TILE : (i + 1) * TILE] = block.T
    rows_ref[...] = start_ref[...].T

    def step(_, carry):
        product_ref[...] = contract(rows_ref[...], acc[...], 1, 0)
        m_ref[...] = contract(product_ref[...], product_ref[...], 1, 1)
        inverse_cholesky(m_ref, v_ref, spread_ref)
        rows_ref[...] = contract(v_ref[...], product_ref[...], 1, 0)
        return carry

    lax.fori_loop(0, ITERS, step, 0)
    basis = three_products(rows_ref[...], True)
    basis_ref[...] = rows_ref[...].T

    for copies in exchange + [kept]:
        for copy in copies:
            copy.wait()
    stores = []
    for i in range(held):
        for lo in range(0, moved.shape[1], STRIPE):
            n = len(stores)
            staged[n] = lax.dot_general(
                three_products(moved[i, lo : lo + STRIPE, :], False),
                basis,
                (((1,), (1,)), ((), ())),
                preferred_element_type=jnp.float32,
            )
            stores.append(pltpu.make_async_copy(staged.at[n], out_ref.at[i, pl.ds(lo, STRIPE), :], store_sem.at[n]))
            stores[n].start()
    for store in stores:
        store.wait()


def on_device(slab, start):
    count, points, columns = slab.shape
    rank = start.shape[1]
    side = lax.axis_size("grp")
    peers = lax.axis_size(DEV)
    held = points // peers
    scale = 1.0 / (count * points * side * peers)
    tiles = columns // TILE
    half = tiles * (tiles + 1) // 4
    stripes = held * count * peers // STRIPE
    slots = 1 + 3 * (side * side - 1) + side
    vmem = pl.BlockSpec(memory_space=pltpu.VMEM)
    hbm = pl.BlockSpec(memory_space=pl.ANY)

    def scratch(*shape):
        return pltpu.VMEM(shape, jnp.float32)

    return pl.pallas_call(
        functools.partial(truncate, side, scale),
        out_shape=(
            jax.ShapeDtypeStruct((held, count * peers, rank), jnp.float32),
            jax.ShapeDtypeStruct((columns, rank), jnp.float32),
        ),
        in_specs=[hbm, vmem],
        out_specs=(hbm, vmem),
        scratch_shapes=[
            scratch(CHUNKS, count // CHUNKS, points, columns),
            scratch(columns, columns),
            scratch(2 * half, TILE, TILE),
            scratch(half, TILE, TILE),
            scratch(half, TILE, TILE),
            scratch(side * side - 1, half, 8, TILE),
            scratch(side, half, 8, TILE),
            scratch(2 * half, TILE, TILE),
            scratch(rank, columns),
            scratch(rank, columns),
            scratch(rank, rank),
            scratch(rank, rank),
            scratch(PANEL + PANEL // 4, 8, 2 * BLOCK),
            scratch(held, count * peers, columns),
            scratch(stripes, STRIPE, rank),
            pltpu.SemaphoreType.DMA((CHUNKS,)),
            pltpu.SemaphoreType.DMA((stripes,)),
            pltpu.SemaphoreType.DMA((held,)),
            pltpu.SemaphoreType.DMA((slots,)),
            pltpu.SemaphoreType.DMA((slots,)),
            pltpu.SemaphoreType.DMA((peers - 1, held)),
            pltpu.SemaphoreType.DMA((peers - 1, held)),
        ],
        compiler_params=pltpu.CompilerParams(
            collective_id=0, has_side_effects=True, vmem_limit_bytes=40 * 1024 * 1024
        ),
        name="truncate",
    )(slab, start)


def solution(mesh):
    torus = Mesh(mesh.devices.reshape(mesh.shape["grp"], 4, 4, 2), AXES)
    return jax.shard_map(
        on_device,
        mesh=torus,
        in_specs=(P(AXES, None, None), P()),
        out_specs=(P(DEV, "grp", None), P()),
        check_vma=False,
    )
```

time: 103 us -> 88.3 us (0.86)
  Pallas kernels: 102 us -> 82.2 us
  local copies, waits for them, and re-layouts: 0.8 us -> 5.34 us
    pallas_call x3 -> x1, Pallas kernels: 102 us -> 82.2 us  [on_device(): pl.pallas_call(functools.partial(truncate, side, scale), out_shape=(jax.S...]
    unnamed x3 -> x6, local copies, waits for them, and re-layouts: 0.8 us -> 5.34 us
where the time goes in v5:
time: 88.3 us; the launch traced here: 88.2 us
  Pallas kernels  82.2 us (93%)
  local copies, waits for them, and re-layouts  5.34 us (6%)
    pallas_call x1, Pallas kernels, on_device(): pl.pallas_call(functools.partial(truncate, side, scale), out_shape=(jax.S...  82.2 us
    unnamed x6, local copies, waits for them, and re-layouts  5.34 us

profile of v5, /device:TPU:1, one launch (start us, length us, event | category | flops | bytes accessed | tf_op | source)
XLA Modules:
  0.0 88.2 jit_solution(11673156727369182881)
XLA Ops:
  0.6 0.0 copy-start
  0.6 2.2 %copy-done = f32[32,64,512]{2,1,0:T(8,128)S(1)} copy-done((f32[32,64,512]{2,1,0:T(8,128)S(1)}, f32[32,64,512]{2,1,0:T(8,128)}, u32[]{:S(2)}) %copy-start) | copy-done | bytes 4194328
  2.8 0.0 copy-start.1
  2.8 1.0 %copy-done.1 = f32[512,256]{1,0:T(8,128)S(1)} copy-done((f32[512,256]{1,0:T(8,128)S(1)}, f32[512,256]{1,0:T(8,128)}, u32[]{:S(2)}) %copy-start.1) | copy-done | bytes 524312
  3.9 82.2 %truncate.1 = (f32[2,1024,256]{2,1,0:T(8,128)S(1)}, f32[512,256]{1,0:T(8,128)S(1)}) custom-call(f32[32,64,512]{2,1,0:T(8,128)S(1)} %copy-done, f32[512,256]{1,0:T(8,128)S(1)} %copy-done.1), custom_call_target="tpu_custom_call" | custom-call | tf_op jit(solution)/shard_map/truncate/pallas_call | solution.py:350
  86.0 1.3 %copy.6 = f32[2,1024,256]{2,1,0:T(8,128)} copy(f32[2,1024,256]{2,1,0:T(8,128)S(1)} %get-tuple-element.4) | data formatting | bytes 4194304
  87.4 0.8 copy.7
Async XLA Ops:
  0.6 2.2 %copy-start = (f32[32,64,512]{2,1,0:T(8,128)S(1)}, f32[32,64,512]{2,1,0:T(8,128)}, u32[]{:S(2)}) copy-start(f32[32,64,512]{2,1,0:T(8,128)} %slab_ref.1) | copy-start | bytes 12582916
  2.8 1.0 %copy-start.1 = (f32[512,256]{1,0:T(8,128)S(1)}, f32[512,256]{1,0:T(8,128)}, u32[]{:S(2)}) copy-start(f32[512,256]{1,0:T(8,128)} %start_ref.1) | copy-start | bytes 1572868

commit v6 on v5

v6 whole, which is shorter than its diff:
```python
import functools

import jax
import jax.numpy as jnp
from jax import lax
from jax.experimental import pallas as pl
from jax.experimental.pallas import tpu as pltpu
from jax.sharding import Mesh
from jax.sharding import PartitionSpec as P

ITERS = 4
DEV = ("dev_0", "dev_1", "dev_2")
AXES = ("grp", *DEV)
MESH = pl.DeviceIdType.MESH
HIGHEST = lax.Precision.HIGHEST
BLOCK = 64
PANEL = 16
TILE = 128
CHUNKS = 4
STRIPE = 256
DURING = (4,)
RAW = (2, 1)
LATE = (3,)


def contract(a, b, dim_a, dim_b):
    return lax.dot_general(
        a, b, (((dim_a,), (dim_b,)), ((), ())), precision=HIGHEST, preferred_element_type=jnp.float32
    )


def inverse_factor(block, spread_ref):
    size = block.shape[0]
    diagonal = lax.broadcasted_iota(jnp.int32, (size, size), 0) == lax.broadcasted_iota(jnp.int32, (size, size), 1)
    both = jnp.concatenate([block, diagonal.astype(jnp.float32)], axis=1)
    wide = (8, 2 * size)
    count = size // 8
    tiles = [both[8 * t : 8 * t + 8, :] for t in range(count)]
    row_of = lax.broadcasted_iota(jnp.int32, wide, 0)

    def over_rows(row):
        return jnp.broadcast_to(row, wide)

    for first in range(0, count, PANEL // 8):
        after = first + PANEL // 8
        cols = [
            [jnp.broadcast_to(tiles[u][:, 8 * first + c : 8 * first + c + 1], wide) for u in range(first, count)]
            for c in range(PANEL)
        ]
        for t in range(first, after):
            spread_ref[PANEL + t - first] = tiles[t]
        spread_ref[0] = cols[0][0]
        for t in range(1, PANEL // 8):
            spread_ref[PANEL + PANEL // 8 + t - 1] = cols[0][t]
        rows = [over_rows(spread_ref[PANEL + i // 8, i % 8 : i % 8 + 1, :]) for i in range(PANEL)]
        pivots, scaled = [], []
        for c in range(PANEL):
            def at(i):
                if c == 0:
                    slot = 0 if i < 8 else PANEL + PANEL // 8 + i // 8 - 1
                    return over_rows(spread_ref[slot, i % 8 : i % 8 + 1, :])
                return over_rows(cols[c][i // 8][i % 8 : i % 8 + 1, :])

            pivots.append(at(c))
            inverse = 1.0 / pivots[c]
            for k in range(c + 1, PANEL):
                factor = at(k) * inverse
                for u in range(k // 8, count - first):
                    cols[k][u] = cols[k][u] - factor * cols[c][u]
                rows[k] = rows[k] - factor * rows[c]
            scaled.append(rows[c] * inverse)
        for u in range(after, count):
            change = cols[0][u - first] * scaled[0]
            for c in range(1, PANEL):
                change = change + cols[c][u - first] * scaled[c]
            tiles[u] = tiles[u] - change
        for c in range(PANEL):
            t = first + c // 8
            tiles[t] = jnp.where(row_of == c % 8, rows[c] * lax.rsqrt(pivots[c]), tiles[t])
    return jnp.concatenate(tiles, axis=0)[:, size:]


def inverse_cholesky(m_ref, v_ref, spread_ref):
    size = m_ref.shape[0]
    v_ref[...] = jnp.zeros_like(v_ref)
    corner = m_ref[:BLOCK, :BLOCK]
    for lo in range(0, size, BLOCK):
        hi = lo + BLOCK
        end = min(hi + BLOCK, size)
        inner = inverse_factor(corner, spread_ref)
        if hi < size:
            across = contract(inner, m_ref[lo:hi, hi:end], 1, 0)
            down = contract(m_ref[hi:end, lo:hi], inner, 1, 1)
            corner = m_ref[hi:end, hi:end] - contract(down, across, 1, 0)
        if lo:
            v_ref[lo:hi, :lo] = contract(inner, v_ref[lo:hi, :lo], 1, 0)
        v_ref[lo:hi, lo:hi] = inner
        if end < size:
            far_across = contract(inner, m_ref[lo:hi, end:], 1, 0)
            far_down = contract(m_ref[end:, lo:hi], inner, 1, 1)
            m_ref[hi:end, end:] -= contract(down, far_across, 1, 0)
            m_ref[end:, hi:end] -= contract(far_down, across, 1, 0)
            m_ref[end:, end:] -= contract(far_down, far_across, 1, 0)
            v_ref[end:, :hi] -= contract(far_down, v_ref[lo:hi, :hi], 1, 0)
        if hi < size:
            v_ref[hi:end, :hi] -= contract(down, v_ref[lo:hi, :hi], 1, 0)


def offsets_at(side, distances):
    def hops(offset):
        return sum(min(step, side - step) for step in offset)

    order = []
    for distance in distances:
        for dx in range(side):
            for dz in range(side):
                if hops((dx, dz)) != distance:
                    continue
                back_x, back_z = (side - dx) % side, (side - dz) % side
                for offset in ((dx, dz), (back_x, back_z), (dz, back_x), (back_z, dx)):
                    if offset not in order:
                        order.append(offset)
    return order


def halves_of(x):
    high = x.astype(jnp.bfloat16)
    return high, (x - high.astype(jnp.float32)).astype(jnp.bfloat16)


def three_products(x, across):
    high, low = halves_of(x)
    return jnp.concatenate([high, low, high] if across else [high, high, low], axis=1)


def truncate(
    side,
    scale,
    slab_ref,
    start_ref,
    moved,
    rows_ref,
    v_ref,
    slab,
    acc,
    part,
    pair,
    mine,
    first_in,
    partial,
    second_in,
    line,
    whole,
    start_held,
    product_ref,
    m_ref,
    spread_ref,
    late_rows,
    late_out,
    load_sem,
    own_sem,
    late_sem,
    sum_send,
    sum_recv,
    row_send,
    row_recv,
):
    y, x, z, core = (lax.axis_index(name) for name in AXES)
    rank, columns = rows_ref.shape
    tiles = columns // TILE
    blocks = [(i, j) for i in range(tiles) for j in range(i, tiles)]
    half = len(blocks) // 2
    count = slab_ref.shape[0]
    held = moved.shape[0]
    depth = count // CHUNKS
    wide = TILE // side
    thin = wide // side

    loads = [
        pltpu.make_async_copy(slab_ref.at[pl.ds(n * depth, depth)], slab.at[n], load_sem.at[n]) for n in range(CHUNKS)
    ]
    loads.append(pltpu.make_async_copy(start_ref, start_held, load_sem.at[CHUNKS]))
    for load in loads:
        load.start()

    first, second = x + core * (z - x), z + core * (x - z)

    def in_plane(f, s):
        return f + core * (s - f), s + core * (f - s)

    steps = range(1, side)
    along_first = [(y, *in_plane(lax.rem(first + k, side), second), core) for k in steps]
    along_second = [(y, *in_plane(first, lax.rem(second + k, side)), core) for k in steps]
    along_y = [(lax.rem(y + k, side), x, z, core) for k in steps]
    partner = (y, x, z, 1 - core)

    barrier = pltpu.get_barrier_semaphore()
    greeted = [*along_first, *along_second, *along_y, partner]
    for to in greeted:
        pl.semaphore_signal(barrier, inc=1, device_id=dict(zip(AXES, to)), device_id_type=MESH)

    def rows_of(index, size):
        return pl.ds(pl.multiple_of(index * size, size), size)

    def number(to):
        return (to[1] * side + to[2]) * 2 + to[3]

    me = number((y, x, z, core))

    def chip(offset):
        step_x, step_z = (step + core * ((side - step) % side - step) for step in offset)
        return lax.rem(x + step_x, side), lax.rem(z + step_z, side)

    def both_cores(distances):
        return [(y, *chip(offset), c) for offset in offsets_at(side, distances) for c in (core, 1 - core)]

    groups = {name: both_cores(name) for name in (DURING, RAW, LATE)}
    groups[()] = [partner]
    exchange, kept, late = {}, [], []
    slot = 0
    for name, peers in groups.items():
        exchange[name] = []
        for n, to in enumerate(peers):
            for i in range(held):
                point = number(to) * held + i
                src, dst = slab_ref.at[:, point, :], moved.at[i, rows_of(me, count), :]
                if name == LATE:
                    place = pl.ds((n * held + i) * count, count)
                    late.append(pltpu.make_async_copy(src, late_rows.at[place], late_sem.at[n, i]))
                    src, dst = late_out.at[place], moved.at[i, rows_of(me, count), pl.ds(0, rank)]
                exchange[name].append(
                    pltpu.make_async_remote_copy(
                        src_ref=src,
                        dst_ref=dst,
                        send_sem=row_send.at[slot, i],
                        recv_sem=row_recv.at[slot, i],
                        device_id=dict(zip(AXES, to)),
                        device_id_type=MESH,
                    )
                )
            slot += 1
    for i in range(held):
        kept.append(
            pltpu.make_async_copy(slab_ref.at[:, me * held + i, :], moved.at[i, rows_of(me, count), :], own_sem.at[i])
        )

    def start(copies):
        for copy in copies:
            copy.start()

    for n in range(CHUNKS):
        loads[n].wait()
        high, low = halves_of(slab[n].reshape(-1, columns))
        for left, right, rows, lo in (
            (high[:, :256], high[:, :256], 256, 0),
            (high, high[:, 256:], columns, 256),
            (high, low, columns, columns),
        ):
            new = lax.dot_general(left, right, (((0,), (0,)), ((), ())), preferred_element_type=jnp.float32)
            place = (slice(0, rows), slice(lo, lo + new.shape[1]))
            acc[place] = acc[place] + new if n else new
    for n, (i, j) in enumerate(blocks):
        across = acc[i * TILE : (i + 1) * TILE, columns + j * TILE : columns + (j + 1) * TILE]
        down = acc[j * TILE : (j + 1) * TILE, columns + i * TILE : columns + (i + 1) * TILE]
        part[n] = (acc[i * TILE : (i + 1) * TILE, j * TILE : (j + 1) * TILE] + (across + down.T)) * scale
    pl.semaphore_wait(barrier, len(greeted))

    slots = iter(range(sum_send.shape[0]))

    def send(src, dst, to):
        slot = next(slots)
        copy = pltpu.make_async_remote_copy(
            src_ref=src,
            dst_ref=dst,
            send_sem=sum_send.at[slot],
            recv_sem=sum_recv.at[slot],
            device_id=dict(zip(AXES, to)),
            device_id_type=MESH,
        )
        copy.start()
        return copy

    def wait(copies):
        for copy in copies:
            copy.wait()

    send(part.at[pl.ds((1 - core) * half, half)], pair, partner).wait()
    own_half = pl.ds(core * half, half)
    mine[...] = part[own_half] + pair[...]

    copies = [
        send(mine.at[:, rows_of(lax.rem(first + k, side), wide), :], first_in.at[k - 1], to)
        for k, to in zip(steps, along_first)
    ]
    start(kept + exchange[()] + late)
    wait(copies)
    partial[...] = mine[:, rows_of(first, wide), :] + (first_in[0] + sum(first_in[k] for k in range(1, side - 1)))
    copies = [
        send(partial.at[:, rows_of(lax.rem(second + k, side), thin), :], second_in.at[k - 1], to)
        for k, to in zip(steps, along_second)
    ]
    wait(copies)
    line[y] = partial[:, rows_of(second, thin), :] + (
        second_in[0] + sum(second_in[k] for k in range(1, side - 1))
    )

    copies = [send(line.at[y], line.at[y], to) for to in along_y]
    start(exchange[DURING])
    wait(copies)
    total = line[0]
    for k in steps:
        total = total + line[k]
    own = whole.at[own_half, rows_of(first * side + second, thin), :]
    own[...] = total

    wait([send(own, own, to) for to in along_second])

    def strip(f):
        return whole.at[own_half, rows_of(f, wide), :]

    copies = [send(strip(first), strip(first), to) for to in along_first]
    passed = [send(strip(first), strip(first), partner)]
    for k, copy in zip(steps, copies):
        copy.wait_recv()
        piece = strip(lax.rem(first + side - k, side))
        passed.append(send(piece, piece, partner))
    for copy in copies:
        copy.wait_send()
    start(exchange[RAW])
    wait(passed)

    for n, (i, j) in enumerate(blocks):
        block = whole[n]
        acc[i * TILE : (i + 1) * TILE, j * TILE : (j + 1) * TILE] = block
        if i != j:
            acc[j * TILE : (j + 1) * TILE, i * TILE : (i + 1) * TILE] = block.T
    loads[CHUNKS].wait()
    rows_ref[...] = start_held[...].T

    def step(k, carry):
        product_ref[...] = contract(rows_ref[...], acc[:, :columns], 1, 0)

        @pl.when(k == ITERS - 1)
        def _():
            wait(late)
            late_out[...] = contract(late_rows[...], product_ref[...], 1, 1)
            start(exchange[LATE])

        m_ref[...] = contract(product_ref[...], product_ref[...], 1, 1)
        inverse_cholesky(m_ref, v_ref, spread_ref)
        rows_ref[...] = contract(v_ref[...], product_ref[...], 1, 0)
        return carry

    lax.fori_loop(0, ITERS, step, 0)
    for copies in exchange.values():
        wait(copies)
    wait(kept)


def project(side, moved_ref, rows_ref, v_ref, out_ref, basis_ref, staged, turned, store_sem):
    x, z = (lax.axis_index(name) for name in DEV[:2])
    held, count, rank = staged.shape
    turned[...] = rows_ref[...].T
    stores = [pltpu.make_async_copy(turned, basis_ref, store_sem.at[0])]
    stores[0].start()
    basis = three_products(rows_ref[...], True)
    stripes = [(i, pl.ds(lo, STRIPE)) for i in range(held) for lo in range(0, count, STRIPE)]
    for i, rows in stripes:
        staged[i, rows, :] = lax.dot_general(
            three_products(moved_ref[i, rows, :], False),
            basis,
            (((1,), (1,)), ((), ())),
            preferred_element_type=jnp.float32,
        )
    size = count // (side * side)
    places = []
    for dx, dz in offsets_at(side, LATE):
        chip = lax.rem(x + dx, side) * side + lax.rem(z + dz, side)
        places += [(i, pl.ds(pl.multiple_of(chip * size, size), size)) for i in range(held)]
    late = jnp.concatenate([moved_ref[i, rows, :rank] for i, rows in places], axis=0)
    late = contract(late, v_ref[...], 1, 1)
    for n, (i, rows) in enumerate(places):
        staged[i, rows, :] = late[n * size : (n + 1) * size]
    for n, (i, rows) in enumerate(stripes):
        stores.append(pltpu.make_async_copy(staged.at[i, rows, :], out_ref.at[i, rows, :], store_sem.at[n + 1]))
        stores[-1].start()
    for store in stores:
        store.wait()


def on_device(slab, start):
    count, points, columns = slab.shape
    rank = start.shape[1]
    side = lax.axis_size("grp")
    peers = lax.axis_size(DEV)
    held = points // peers
    scale = 1.0 / (count * points * side * peers)
    tiles = columns // TILE
    half = tiles * (tiles + 1) // 4
    late = 2 * len(offsets_at(side, LATE))
    slots = 1 + 5 * (side - 1) + side
    vmem = pl.BlockSpec(memory_space=pltpu.VMEM)
    hbm = pl.BlockSpec(memory_space=pltpu.HBM)

    def scratch(*shape):
        return pltpu.VMEM(shape, jnp.float32)

    moved, rows, factor = pl.pallas_call(
        functools.partial(truncate, side, scale),
        out_shape=(
            jax.ShapeDtypeStruct((held, count * peers, columns), jnp.float32),
            jax.ShapeDtypeStruct((rank, columns), jnp.float32),
            jax.ShapeDtypeStruct((rank, rank), jnp.float32),
        ),
        in_specs=[hbm, hbm],
        out_specs=(vmem, vmem, vmem),
        scratch_shapes=[
            scratch(CHUNKS, count // CHUNKS, points, columns),
            scratch(columns, 2 * columns),
            scratch(2 * half, TILE, TILE),
            scratch(half, TILE, TILE),
            scratch(half, TILE, TILE),
            scratch(side - 1, half, TILE // side, TILE),
            scratch(half, TILE // side, TILE),
            scratch(side - 1, half, TILE // side**2, TILE),
            scratch(side, half, TILE // side**2, TILE),
            scratch(2 * half, TILE, TILE),
            scratch(columns, rank),
            scratch(rank, columns),
            scratch(rank, rank),
            scratch(PANEL + PANEL // 4, 8, 2 * BLOCK),
            scratch(late * held * count, columns),
            scratch(late * held * count, rank),
            pltpu.SemaphoreType.DMA((CHUNKS + 1,)),
            pltpu.SemaphoreType.DMA((held,)),
            pltpu.SemaphoreType.DMA((late, held)),
            pltpu.SemaphoreType.DMA((slots,)),
            pltpu.SemaphoreType.DMA((slots,)),
            pltpu.SemaphoreType.DMA((peers - 1, held)),
            pltpu.SemaphoreType.DMA((peers - 1, held)),
        ],
        compiler_params=pltpu.CompilerParams(
            collective_id=0, has_side_effects=True, vmem_limit_bytes=47 * 1024 * 1024
        ),
        name="truncate",
    )(slab, start)
    return pl.pallas_call(
        functools.partial(project, side),
        out_shape=(
            jax.ShapeDtypeStruct((held, count * peers, rank), jnp.float32),
            jax.ShapeDtypeStruct((columns, rank), jnp.float32),
        ),
        in_specs=[vmem, vmem, vmem],
        out_specs=(hbm, hbm),
        scratch_shapes=[
            scratch(held, count * peers, rank),
            scratch(columns, rank),
            pltpu.SemaphoreType.DMA((1 + held * count * peers // STRIPE,)),
        ],
        compiler_params=pltpu.CompilerParams(vmem_limit_bytes=24 * 1024 * 1024),
        name="project",
    )(moved, rows, factor)


def solution(mesh):
    torus = Mesh(mesh.devices.reshape(mesh.shape["grp"], 4, 4, 2), AXES)
    return jax.shard_map(
        on_device,
        mesh=torus,
        in_specs=(P(AXES, None, None), P()),
        out_specs=(P(DEV, "grp", None), P()),
        check_vma=False,
    )
```

time: 88.3 us -> 90.4 us (1.024)
  Pallas kernels: 82.2 us -> 88.4 us
  local copies, waits for them, and re-layouts: 5.34 us -> 1.03 us
    unnamed x6 -> x2, local copies, waits for them, and re-layouts: 5.34 us -> 1.03 us
    pallas_call x0 -> x1, Pallas kernels: none -> 3.75 us  [on_device(): pl.pallas_call(functools.partial(project, side), out_shape=(jax.ShapeDtyp...]
    pallas_call x1, Pallas kernels: 82.2 us -> 84.7 us  [on_device(): pl.pallas_call(functools.partial(truncate, side, scale), out_shape=(jax.S...]
where the time goes in v6:
time: 90.4 us; the launch traced here: 90.3 us
  Pallas kernels  88.4 us (98%)
  local copies, waits for them, and re-layouts  1.03 us (1%)
    pallas_call x1, Pallas kernels, on_device(): pl.pallas_call(functools.partial(truncate, side, scale), out_shape=(jax.S...  84.7 us
    pallas_call x1, Pallas kernels, on_device(): pl.pallas_call(functools.partial(project, side), out_shape=(jax.ShapeDtyp...  3.75 us

profile of v6, /device:TPU:1, one launch (start us, length us, event | category | flops | bytes accessed | tf_op | source)
XLA Modules:
  0.0 90.3 jit_solution(11476769367409159994)
XLA Ops:
  0.6 0.0 copy-start
  0.6 1.0 %copy-done = f32[512,256]{1,0:T(8,128)S(1)} copy-done((f32[512,256]{1,0:T(8,128)S(1)}, f32[512,256]{1,0:T(8,128)}, u32[]{:S(2)}) %copy-start) | copy-done | bytes 524312
  1.7 84.7 %truncate.1 = (f32[2,1024,512]{2,1,0:T(8,128)S(1)}, f32[256,512]{1,0:T(8,128)S(1)}, f32[256,256]{1,0:T(8,128)S(1)}) custom-call(f32[32,64,512]{2,1,0:T(8,128)} %slab_ref.1, f32[512,256]{1,0:T(8,128)S(1)} %copy-done), custom_call_target="tpu_custom_call" | custom-call | tf_op jit(solution)/shard_map/truncate/pallas_call | solution.py:408
  86.3 3.8 %project.1 = (f32[2,1024,256]{2,1,0:T(8,128)}, f32[512,256]{1,0:T(8,128)}) custom-call(f32[2,1024,512]{2,1,0:T(8,128)S(1)} %get-tuple-element.5.moved_ref, f32[256,512]{1,0:T(8,128)S(1)} %get-tuple-element.6.rows_ref, f32[256,256]{1,0:T(8,128)S(1)} %get-tuple-element.7.v_ref), custom_call_target="tpu_custom_call" | custom-call | tf_op jit(solution)/shard_map/project/pallas_call | solution.py:447
Async XLA Ops:
  0.6 1.0 %copy-start = (f32[512,256]{1,0:T(8,128)S(1)}, f32[512,256]{1,0:T(8,128)}, u32[]{:S(2)}) copy-start(f32[512,256]{1,0:T(8,128)} %start_ref.1) | copy-start | bytes 1572868

commit v7 on v6

--- a/solution.py
+++ b/solution.py
@@ -18,9 +18,13 @@
 TILE = 128
 CHUNKS = 4
 STRIPE = 256
-DURING = (4,)
-RAW = (2, 1)
-LATE = (3,)
+
+
+def short_contract(a, b, dim_a, dim_b):
+    (a, a_low), (b, b_low) = halves_of(a), halves_of(b)
+    dims = (((dim_a,), (dim_b,)), ((), ()))
+    products = [lax.dot_general(p, q, dims, preferred_element_type=jnp.float32) for p, q in ((a, b), (a, b_low), (a_low, b))]
+    return products[0] + (products[1] + products[2])
 
 
 def contract(a, b, dim_a, dim_b):
@@ -106,21 +110,26 @@
             v_ref[hi:end, :hi] -= contract(down, v_ref[lo:hi, :hi], 1, 0)
 
 
-def offsets_at(side, distances):
-    def hops(offset):
-        return sum(min(step, side - step) for step in offset)
-
+def offsets_at(side, distance):
     order = []
-    for distance in distances:
-        for dx in range(side):
-            for dz in range(side):
-                if hops((dx, dz)) != distance:
-                    continue
-                back_x, back_z = (side - dx) % side, (side - dz) % side
-                for offset in ((dx, dz), (back_x, back_z), (dz, back_x), (back_z, dx)):
-                    if offset not in order:
-                        order.append(offset)
+    for dx in range(side):
+        for dz in range(side):
+            if min(dx, side - dx) + min(dz, side - dz) != distance:
+                continue
+            back_x, back_z = (side - dx) % side, (side - dz) % side
+            for offset in ((dx, dz), (back_x, back_z), (dz, back_x), (back_z, dx)):
+                if offset not in order:
+                    order.append(offset)
     return order
+
+
+def late_offsets(side):
+    return [(offset, 0) for offset in offsets_at(side, 3)] + [(offset, 1) for offset in offsets_at(side, 4)]
+
+
+def raw_offsets(side):
+    every = [(offset, flip) for d in (4, 3, 2, 1) for offset in offsets_at(side, d) for flip in range(2)]
+    return [(offset, flip) for offset, flip in every if (offset, flip) not in late_offsets(side)]
 
 
 def halves_of(x):
@@ -148,8 +157,7 @@
     mine,
     first_in,
     partial,
-    second_in,
-    line,
+    slices,
     whole,
     start_held,
     product_ref,
@@ -191,11 +199,12 @@
     steps = range(1, side)
     along_first = [(y, *in_plane(lax.rem(first + k, side), second), core) for k in steps]
     along_second = [(y, *in_plane(first, lax.rem(second + k, side)), core) for k in steps]
-    along_y = [(lax.rem(y + k, side), x, z, core) for k in steps]
+    around = [(ky, ks) for ky in range(side) for ks in range(side) if ky or ks]
+    crossing = [(lax.rem(y + ky, side), *in_plane(first, lax.rem(second + ks, side)), core) for ky, ks in around]
     partner = (y, x, z, 1 - core)
 
     barrier = pltpu.get_barrier_semaphore()
-    greeted = [*along_first, *along_second, *along_y, partner]
+    greeted = [*along_first, *crossing, partner]
     for to in greeted:
         pl.semaphore_signal(barrier, inc=1, device_id=dict(zip(AXES, to)), device_id_type=MESH)
 
@@ -211,11 +220,10 @@
         step_x, step_z = (step + core * ((side - step) % side - step) for step in offset)
         return lax.rem(x + step_x, side), lax.rem(z + step_z, side)
 
-    def both_cores(distances):
-        return [(y, *chip(offset), c) for offset in offsets_at(side, distances) for c in (core, 1 - core)]
-
-    groups = {name: both_cores(name) for name in (DURING, RAW, LATE)}
-    groups[()] = [partner]
+    def devices(offsets):
+        return [(y, *chip(offset), core + flip * (1 - 2 * core)) for offset, flip in offsets]
+
+    groups = {"near": [partner], "raw": devices(raw_offsets(side)), "late": devices(late_offsets(side))}
     exchange, kept, late = {}, [], []
     slot = 0
     for name, peers in groups.items():
@@ -224,7 +232,7 @@
             for i in range(held):
                 point = number(to) * held + i
                 src, dst = slab_ref.at[:, point, :], moved.at[i, rows_of(me, count), :]
-                if name == LATE:
+                if name == "late":
                     place = pl.ds((n * held + i) * count, count)
                     late.append(pltpu.make_async_copy(src, late_rows.at[place], late_sem.at[n, i]))
                     src, dst = late_out.at[place], moved.at[i, rows_of(me, count), pl.ds(0, rank)]
@@ -265,26 +273,32 @@
         part[n] = (acc[i * TILE : (i + 1) * TILE, j * TILE : (j + 1) * TILE] + (across + down.T)) * scale
     pl.semaphore_wait(barrier, len(greeted))
 
-    slots = iter(range(sum_send.shape[0]))
+    sent = []
 
     def send(src, dst, to):
-        slot = next(slots)
-        copy = pltpu.make_async_remote_copy(
-            src_ref=src,
-            dst_ref=dst,
-            send_sem=sum_send.at[slot],
-            recv_sem=sum_recv.at[slot],
-            device_id=dict(zip(AXES, to)),
-            device_id_type=MESH,
+        slot = len(sent)
+        sent.append(
+            pltpu.make_async_remote_copy(
+                src_ref=src,
+                dst_ref=dst,
+                send_sem=sum_send.at[slot],
+                recv_sem=sum_recv.at[slot],
+                device_id=dict(zip(AXES, to)),
+                device_id_type=MESH,
+            )
         )
-        copy.start()
-        return copy
+        sent[slot].start()
+        return sent[slot]
+
+    def arrive(copies):
+        for copy in copies:
+            copy.wait_recv()
 
     def wait(copies):
         for copy in copies:
             copy.wait()
 
-    send(part.at[pl.ds((1 - core) * half, half)], pair, partner).wait()
+    arrive([send(part.at[pl.ds((1 - core) * half, half)], pair, partner)])
     own_half = pl.ds(core * half, half)
     mine[...] = part[own_half] + pair[...]
 
@@ -292,28 +306,23 @@
         send(mine.at[:, rows_of(lax.rem(first + k, side), wide), :], first_in.at[k - 1], to)
         for k, to in zip(steps, along_first)
     ]
-    start(kept + exchange[()] + late)
-    wait(copies)
+    start(kept + exchange["near"] + late)
+    arrive(copies)
     partial[...] = mine[:, rows_of(first, wide), :] + (first_in[0] + sum(first_in[k] for k in range(1, side - 1)))
+    source = y * side + second
     copies = [
-        send(partial.at[:, rows_of(lax.rem(second + k, side), thin), :], second_in.at[k - 1], to)
-        for k, to in zip(steps, along_second)
+        send(partial.at[:, rows_of(lax.rem(second + ks, side), thin), :], slices.at[source], to)
+        for (_, ks), to in zip(around, crossing)
     ]
-    wait(copies)
-    line[y] = partial[:, rows_of(second, thin), :] + (
-        second_in[0] + sum(second_in[k] for k in range(1, side - 1))
-    )
-
-    copies = [send(line.at[y], line.at[y], to) for to in along_y]
-    start(exchange[DURING])
-    wait(copies)
-    total = line[0]
-    for k in steps:
-        total = total + line[k]
+    slices[source] = partial[:, rows_of(second, thin), :]
+    arrive(copies)
+    total = slices[0]
+    for k in range(1, side * side):
+        total = total + slices[k]
     own = whole.at[own_half, rows_of(first * side + second, thin), :]
     own[...] = total
 
-    wait([send(own, own, to) for to in along_second])
+    arrive([send(own, own, to) for to in along_second])
 
     def strip(f):
         return whole.at[own_half, rows_of(f, wide), :]
@@ -324,10 +333,8 @@
         copy.wait_recv()
         piece = strip(lax.rem(first + side - k, side))
         passed.append(send(piece, piece, partner))
-    for copy in copies:
-        copy.wait_send()
-    start(exchange[RAW])
-    wait(passed)
+    start(exchange["raw"])
+    arrive(passed)
 
     for n, (i, j) in enumerate(blocks):
         block = whole[n]
@@ -343,22 +350,24 @@
         @pl.when(k == ITERS - 1)
         def _():
             wait(late)
-            late_out[...] = contract(late_rows[...], product_ref[...], 1, 1)
-            start(exchange[LATE])
-
-        m_ref[...] = contract(product_ref[...], product_ref[...], 1, 1)
+            late_out[...] = short_contract(late_rows[...], product_ref[...], 1, 1)
+            start(exchange["late"])
+
+        m_ref[...] = short_contract(product_ref[...], product_ref[...], 1, 1)
         inverse_cholesky(m_ref, v_ref, spread_ref)
-        rows_ref[...] = contract(v_ref[...], product_ref[...], 1, 0)
+        rows_ref[...] = short_contract(v_ref[...], product_ref[...], 1, 0)
         return carry
 
     lax.fori_loop(0, ITERS, step, 0)
     for copies in exchange.values():
         wait(copies)
     wait(kept)
+    for copy in sent:
+        copy.wait_send()
 
 
 def project(side, moved_ref, rows_ref, v_ref, out_ref, basis_ref, staged, turned, store_sem):
-    x, z = (lax.axis_index(name) for name in DEV[:2])
+    x, z, core = (lax.axis_index(name) for name in DEV)
     held, count, rank = staged.shape
     turned[...] = rows_ref[...].T
     stores = [pltpu.make_async_copy(turned, basis_ref, store_sem.at[0])]
@@ -372,13 +381,14 @@
             (((1,), (1,)), ((), ())),
             preferred_element_type=jnp.float32,
         )
-    size = count // (side * side)
+    size = count // (2 * side * side)
     places = []
-    for dx, dz in offsets_at(side, LATE):
+    for (dx, dz), flip in late_offsets(side):
         chip = lax.rem(x + dx, side) * side + lax.rem(z + dz, side)
-        places += [(i, pl.ds(pl.multiple_of(chip * size, size), size)) for i in range(held)]
+        device = 2 * chip + core + flip * (1 - 2 * core)
+        places += [(i, pl.ds(pl.multiple_of(device * size, size), size)) for i in range(held)]
     late = jnp.concatenate([moved_ref[i, rows, :rank] for i, rows in places], axis=0)
-    late = contract(late, v_ref[...], 1, 1)
+    late = short_contract(late, v_ref[...], 1, 1)
     for n, (i, rows) in enumerate(places):
         staged[i, rows, :] = late[n * size : (n + 1) * size]
     for n, (i, rows) in enumerate(stripes):
@@ -397,8 +407,8 @@
     scale = 1.0 / (count * points * side * peers)
     tiles = columns // TILE
     half = tiles * (tiles + 1) // 4
-    late = 2 * len(offsets_at(side, LATE))
-    slots = 1 + 5 * (side - 1) + side
+    late = len(late_offsets(side))
+    slots = side * side + 3 * (side - 1) + side
     vmem = pl.BlockSpec(memory_space=pltpu.VMEM)
     hbm = pl.BlockSpec(memory_space=pltpu.HBM)
 
@@ -422,8 +432,7 @@
             scratch(half, TILE, TILE),
             scratch(side - 1, half, TILE // side, TILE),
             scratch(half, TILE // side, TILE),
-            scratch(side - 1, half, TILE // side**2, TILE),
-            scratch(side, half, TILE // side**2, TILE),
+            scratch(side * side, half, TILE // side**2, TILE),
             scratch(2 * half, TILE, TILE),
             scratch(columns, rank),
             scratch(rank, columns),

time: 90.4 us -> 81.7 us (0.904)
  Pallas kernels: 88.4 us -> 79.9 us
    pallas_call x1, Pallas kernels: 84.7 us -> 76.3 us  [on_device(): pl.pallas_call(functools.partial(truncate, side, scale), out_shape=(jax.S...]
where the time goes in v7:
time: 81.7 us; the launch traced here: 81.5 us
  Pallas kernels  79.9 us (98%)
  local copies, waits for them, and re-layouts  1.03 us (1%)
    pallas_call x1, Pallas kernels, on_device(): pl.pallas_call(functools.partial(truncate, side, scale), out_shape=(jax.S...  76.3 us
    pallas_call x1, Pallas kernels, on_device(): pl.pallas_call(functools.partial(project, side), out_shape=(jax.ShapeDtyp...  3.53 us

profile of v7, /device:TPU:1, one launch (start us, length us, event | category | flops | bytes accessed | tf_op | source)
XLA Modules:
  0.0 81.5 jit_solution(17136169893890235316)
XLA Ops:
  0.6 0.0 copy-start
  0.6 1.0 %copy-done = f32[512,256]{1,0:T(8,128)S(1)} copy-done((f32[512,256]{1,0:T(8,128)S(1)}, f32[512,256]{1,0:T(8,128)}, u32[]{:S(2)}) %copy-start) | copy-done | bytes 524312
  1.7 76.3 %truncate.1 = (f32[2,1024,512]{2,1,0:T(8,128)S(1)}, f32[256,512]{1,0:T(8,128)S(1)}, f32[256,256]{1,0:T(8,128)S(1)}) custom-call(f32[32,64,512]{2,1,0:T(8,128)} %slab_ref.1, f32[512,256]{1,0:T(8,128)S(1)} %copy-done), custom_call_target="tpu_custom_call" | custom-call | tf_op jit(solution)/shard_map/truncate/pallas_call | solution.py:418
  78.0 3.5 %project.1 = (f32[2,1024,256]{2,1,0:T(8,128)}, f32[512,256]{1,0:T(8,128)}) custom-call(f32[2,1024,512]{2,1,0:T(8,128)S(1)} %get-tuple-element.5.moved_ref, f32[256,512]{1,0:T(8,128)S(1)} %get-tuple-element.6.rows_ref, f32[256,256]{1,0:T(8,128)S(1)} %get-tuple-element.7.v_ref), custom_call_target="tpu_custom_call" | custom-call | tf_op jit(solution)/shard_map/project/pallas_call | solution.py:456
Async XLA Ops:
  0.6 1.0 %copy-start = (f32[512,256]{1,0:T(8,128)S(1)}, f32[512,256]{1,0:T(8,128)}, u32[]{:S(2)}) copy-start(f32[512,256]{1,0:T(8,128)} %start_ref.1) | copy-start | bytes 1572868

commit v8 on v7

--- a/solution.py
+++ b/solution.py
@@ -124,7 +124,7 @@
 
 
 def late_offsets(side):
-    return [(offset, 0) for offset in offsets_at(side, 3)] + [(offset, 1) for offset in offsets_at(side, 4)]
+    return [(offset, 0) for offset in offsets_at(side, 3)]
 
 
 def raw_offsets(side):
@@ -157,7 +157,8 @@
     mine,
     first_in,
     partial,
-    slices,
+    second_in,
+    line,
     whole,
     start_held,
     product_ref,
@@ -199,12 +200,11 @@
     steps = range(1, side)
     along_first = [(y, *in_plane(lax.rem(first + k, side), second), core) for k in steps]
     along_second = [(y, *in_plane(first, lax.rem(second + k, side)), core) for k in steps]
-    around = [(ky, ks) for ky in range(side) for ks in range(side) if ky or ks]
-    crossing = [(lax.rem(y + ky, side), *in_plane(first, lax.rem(second + ks, side)), core) for ky, ks in around]
+    along_y = [(lax.rem(y + k, side), x, z, core) for k in steps]
     partner = (y, x, z, 1 - core)
 
     barrier = pltpu.get_barrier_semaphore()
-    greeted = [*along_first, *crossing, partner]
+    greeted = [*along_first, *along_second, *along_y, partner]
     for to in greeted:
         pl.semaphore_signal(barrier, inc=1, device_id=dict(zip(AXES, to)), device_id_type=MESH)
 
@@ -223,7 +223,7 @@
     def devices(offsets):
         return [(y, *chip(offset), core + flip * (1 - 2 * core)) for offset, flip in offsets]
 
-    groups = {"near": [partner], "raw": devices(raw_offsets(side)), "late": devices(late_offsets(side))}
+    groups = {"near": [partner], "early": devices(raw_offsets(side)[:2]), "raw": devices(raw_offsets(side)[2:]), "late": devices(late_offsets(side))}
     exchange, kept, late = {}, [], []
     slot = 0
     for name, peers in groups.items():
@@ -309,16 +309,18 @@
     start(kept + exchange["near"] + late)
     arrive(copies)
     partial[...] = mine[:, rows_of(first, wide), :] + (first_in[0] + sum(first_in[k] for k in range(1, side - 1)))
-    source = y * side + second
     copies = [
-        send(partial.at[:, rows_of(lax.rem(second + ks, side), thin), :], slices.at[source], to)
-        for (_, ks), to in zip(around, crossing)
+        send(partial.at[:, rows_of(lax.rem(second + k, side), thin), :], second_in.at[k - 1], to)
+        for k, to in zip(steps, along_second)
     ]
-    slices[source] = partial[:, rows_of(second, thin), :]
     arrive(copies)
-    total = slices[0]
-    for k in range(1, side * side):
-        total = total + slices[k]
+    line[y] = partial[:, rows_of(second, thin), :] + (second_in[0] + sum(second_in[k] for k in range(1, side - 1)))
+    copies = [send(line.at[y], line.at[y], to) for to in along_y]
+    start(exchange["early"])
+    arrive(copies)
+    total = line[0]
+    for k in steps:
+        total = total + line[k]
     own = whole.at[own_half, rows_of(first * side + second, thin), :]
     own[...] = total
 
@@ -353,9 +355,18 @@
             late_out[...] = short_contract(late_rows[...], product_ref[...], 1, 1)
             start(exchange["late"])
 
-        m_ref[...] = short_contract(product_ref[...], product_ref[...], 1, 1)
+        def either(out_ref, a_ref, b_ref, dim_b):
+            @pl.when(k == 0)
+            def _():
+                out_ref[...] = contract(a_ref[...], b_ref[...], 1, dim_b)
+
+            @pl.when(k > 0)
+            def _():
+                out_ref[...] = short_contract(a_ref[...], b_ref[...], 1, dim_b)
+
+        either(m_ref, product_ref, product_ref, 1)
         inverse_cholesky(m_ref, v_ref, spread_ref)
-        rows_ref[...] = short_contract(v_ref[...], product_ref[...], 1, 0)
+        either(rows_ref, v_ref, product_ref, 0)
         return carry
 
     lax.fori_loop(0, ITERS, step, 0)
@@ -408,7 +419,7 @@
     tiles = columns // TILE
     half = tiles * (tiles + 1) // 4
     late = len(late_offsets(side))
-    slots = side * side + 3 * (side - 1) + side
+    slots = 1 + 5 * (side - 1) + side
     vmem = pl.BlockSpec(memory_space=pltpu.VMEM)
     hbm = pl.BlockSpec(memory_space=pltpu.HBM)
 
@@ -432,7 +443,8 @@
             scratch(half, TILE, TILE),
             scratch(side - 1, half, TILE // side, TILE),
             scratch(half, TILE // side, TILE),
-            scratch(side * side, half, TILE // side**2, TILE),
+            scratch(side - 1, half, TILE // side**2, TILE),
+            scratch(side, half, TILE // side**2, TILE),
             scratch(2 * half, TILE, TILE),
             scratch(columns, rank),
             scratch(rank, columns),

time: 81.7 us -> 81.1 us (level)
  no operation moved by 1% of the time
where the time goes in v8:
time: 81.1 us; the launch traced here: 80.9 us
  Pallas kernels  79.1 us (98%)
  local copies, waits for them, and re-layouts  1.03 us (1%)
    pallas_call x1, Pallas kernels, on_device(): pl.pallas_call(functools.partial(truncate, side, scale), out_shape=(jax.S...  75.6 us
    pallas_call x1, Pallas kernels, on_device(): pl.pallas_call(functools.partial(project, side), out_shape=(jax.ShapeDtyp...  3.47 us

profile of v8, /device:TPU:1, one launch (start us, length us, event | category | flops | bytes accessed | tf_op | source)
XLA Modules:
  0.0 80.9 jit_solution(806745992960817636)
XLA Ops:
  0.6 0.0 copy-start
  0.6 1.0 %copy-done = f32[512,256]{1,0:T(8,128)S(1)} copy-done((f32[512,256]{1,0:T(8,128)S(1)}, f32[512,256]{1,0:T(8,128)}, u32[]{:S(2)}) %copy-start) | copy-done | bytes 524312
  1.7 75.6 %truncate.1 = (f32[2,1024,512]{2,1,0:T(8,128)S(1)}, f32[256,512]{1,0:T(8,128)S(1)}, f32[256,256]{1,0:T(8,128)S(1)}) custom-call(f32[32,64,512]{2,1,0:T(8,128)} %slab_ref.1, f32[512,256]{1,0:T(8,128)S(1)} %copy-done), custom_call_target="tpu_custom_call" | custom-call | tf_op jit(solution)/shard_map/truncate/pallas_call | solution.py:429
  77.3 3.5 %project.1 = (f32[2,1024,256]{2,1,0:T(8,128)}, f32[512,256]{1,0:T(8,128)}) custom-call(f32[2,1024,512]{2,1,0:T(8,128)S(1)} %get-tuple-element.5.moved_ref, f32[256,512]{1,0:T(8,128)S(1)} %get-tuple-element.6.rows_ref, f32[256,256]{1,0:T(8,128)S(1)} %get-tuple-element.7.v_ref), custom_call_target="tpu_custom_call" | custom-call | tf_op jit(solution)/shard_map/project/pallas_call | solution.py:468
Async XLA Ops:
  0.6 1.0 %copy-start = (f32[512,256]{1,0:T(8,128)S(1)}, f32[512,256]{1,0:T(8,128)}, u32[]{:S(2)}) copy-start(f32[512,256]{1,0:T(8,128)} %start_ref.1) | copy-start | bytes 1572868

commit v9 on v8

--- a/solution.py
+++ b/solution.py
@@ -84,7 +84,7 @@
     return jnp.concatenate(tiles, axis=0)[:, size:]
 
 
-def inverse_cholesky(m_ref, v_ref, spread_ref):
+def inverse_cholesky(m_ref, v_ref, spread_ref, contract):
     size = m_ref.shape[0]
     v_ref[...] = jnp.zeros_like(v_ref)
     corner = m_ref[:BLOCK, :BLOCK]
@@ -355,18 +355,13 @@
             late_out[...] = short_contract(late_rows[...], product_ref[...], 1, 1)
             start(exchange["late"])
 
-        def either(out_ref, a_ref, b_ref, dim_b):
-            @pl.when(k == 0)
-            def _():
-                out_ref[...] = contract(a_ref[...], b_ref[...], 1, dim_b)
-
-            @pl.when(k > 0)
-            def _():
-                out_ref[...] = short_contract(a_ref[...], b_ref[...], 1, dim_b)
-
-        either(m_ref, product_ref, product_ref, 1)
-        inverse_cholesky(m_ref, v_ref, spread_ref)
-        either(rows_ref, v_ref, product_ref, 0)
+        def orthonormalise(product):
+            m_ref[...] = product(product_ref[...], product_ref[...], 1, 1)
+            inverse_cholesky(m_ref, v_ref, spread_ref, product)
+            rows_ref[...] = product(v_ref[...], product_ref[...], 1, 0)
+
+        pl.when(k == 0)(functools.partial(orthonormalise, contract))
+        pl.when(k > 0)(functools.partial(orthonormalise, short_contract))
         return carry
 
     lax.fori_loop(0, ITERS, step, 0)

time: 81.1 us -> 80.7 us (level)
  no operation moved by 1% of the time
where the time goes in v9:
time: 80.7 us; the launch traced here: 80.6 us
  Pallas kernels  78.7 us (98%)
  local copies, waits for them, and re-layouts  1.03 us (1%)
  between operations  0.83 us (1%)
    pallas_call x1, Pallas kernels, on_device(): pl.pallas_call(functools.partial(truncate, side, scale), out_shape=(jax.S...  75.2 us
    pallas_call x1, Pallas kernels, on_device(): pl.pallas_call(functools.partial(project, side), out_shape=(jax.ShapeDtyp...  3.47 us

profile of v9, /device:TPU:1, one launch (start us, length us, event | category | flops | bytes accessed | tf_op | source)
XLA Modules:
  0.0 80.6 jit_solution(4008916170430644919)
XLA Ops:
  0.6 0.0 copy-start
  0.6 1.0 %copy-done = f32[512,256]{1,0:T(8,128)S(1)} copy-done((f32[512,256]{1,0:T(8,128)S(1)}, f32[512,256]{1,0:T(8,128)}, u32[]{:S(2)}) %copy-start) | copy-done | bytes 524312
  1.7 75.2 %truncate.1 = (f32[2,1024,512]{2,1,0:T(8,128)S(1)}, f32[256,512]{1,0:T(8,128)S(1)}, f32[256,256]{1,0:T(8,128)S(1)}) custom-call(f32[32,64,512]{2,1,0:T(8,128)} %slab_ref.1, f32[512,256]{1,0:T(8,128)S(1)} %copy-done), custom_call_target="tpu_custom_call" | custom-call | tf_op jit(solution)/shard_map/truncate/pallas_call | solution.py:424
  76.9 3.5 %project.1 = (f32[2,1024,256]{2,1,0:T(8,128)}, f32[512,256]{1,0:T(8,128)}) custom-call(f32[2,1024,512]{2,1,0:T(8,128)S(1)} %get-tuple-element.5.moved_ref, f32[256,512]{1,0:T(8,128)S(1)} %get-tuple-element.6.rows_ref, f32[256,256]{1,0:T(8,128)S(1)} %get-tuple-element.7.v_ref), custom_call_target="tpu_custom_call" | custom-call | tf_op jit(solution)/shard_map/project/pallas_call | solution.py:463
Async XLA Ops:
  0.6 1.0 %copy-start = (f32[512,256]{1,0:T(8,128)S(1)}, f32[512,256]{1,0:T(8,128)}, u32[]{:S(2)}) copy-start(f32[512,256]{1,0:T(8,128)} %start_ref.1) | copy-start | bytes 1572868
